TPU v7x, 32 devices: a whole 2x2x4 slice. The times are simulated.
32 devices in a mesh: ctx: 8 (over y, x, core), fsdp: 4 (over z).
Axes of the slice: x: 2, y: 2, z: 4, core: 2. Of those that a mesh axis runs over, the one named last changes fastest.
Arguments:
- block_input: bfloat16 [2, 4, 512, 1536], P(None, 'fsdp', 'ctx'), may hold values from -6 to 6
- positions: int32 [2, 4, 512], P(None, 'fsdp', 'ctx'), may hold values from 0 to 511, as said below
- segments: int32 [2, 4, 512], P(None, 'fsdp', 'ctx'), may hold values from 0 to 2, as said below
- out_cotangent: bfloat16 [2, 4, 512, 1536], P(None, 'fsdp', 'ctx'), may hold values from -6 to 6
- attn_gain: bfloat16 [1536], P(('ctx', 'fsdp')), may hold values from 0.5 to 1.5
- w_query: bfloat16 [1536, 1536], P(('ctx', 'fsdp')), may hold values from -0.15625 to 0.15625
- w_key: bfloat16 [1536, 768], P(('ctx', 'fsdp')), may hold values from -0.15625 to 0.15625
- w_value: bfloat16 [1536, 768], P(('ctx', 'fsdp')), may hold values from -0.15625 to 0.15625
- w_out: bfloat16 [1536, 1536], P(('ctx', 'fsdp')), may hold values from -0.625 to 0.625
- mlp_gain: bfloat16 [1536], P(('ctx', 'fsdp')), may hold values from 0.5 to 1.5
- w_gate: bfloat16 [1536, 4096], P(('ctx', 'fsdp')), may hold values from -0.15625 to 0.15625
- w_up: bfloat16 [1536, 4096], P(('ctx', 'fsdp')), may hold values from -0.15625 to 0.15625
- w_down: bfloat16 [4096, 1536], P(('ctx', 'fsdp')), may hold values from -0.09375 to 0.09375
Outputs:
- block_output: bfloat16 [2, 4, 512, 1536], P(None, 'fsdp', 'ctx')
- input_grad: bfloat16 [2, 4, 512, 1536], P(None, 'fsdp', 'ctx')
- grad_attn_gain: float32 [1536], P(('ctx', 'fsdp'))
- grad_query: float32 [1536, 1536], P(('ctx', 'fsdp'))
- grad_key: float32 [1536, 768], P(('ctx', 'fsdp'))
- grad_value: float32 [1536, 768], P(('ctx', 'fsdp'))
- grad_out: float32 [1536, 1536], P(('ctx', 'fsdp'))
- grad_mlp_gain: float32 [1536], P(('ctx', 'fsdp'))
- grad_gate: float32 [1536, 4096], P(('ctx', 'fsdp'))
- grad_up: float32 [1536, 4096], P(('ctx', 'fsdp'))
- grad_down: float32 [4096, 1536], P(('ctx', 'fsdp'))
Inputs may be any that keep to these rules, and one draw needn't show every extreme that they name: In each sequence every position appears once; the 64 tokens of one index of ctx are 32 consecutive positions starting at c * 32 followed by 32 starting at (15 - c) * 32, for some c below 8. `segments`: ordered by position, segment ids start at 0 and rise by one at each new document, except that the last document of each sequence has the id 512 // 200; every document has 200 to 2000 positions except that the last of a sequence may have fewer.
All inputs are finite; a program needn't handle non-finite values.
Results may differ from a plain program's by a relative error of at most 0.02.
Values may be sent and summed in bfloat16 or wider, within the bound.
No kernel may reach another device: no remote copies, remote signals or barrier semaphores. Data moves between devices by JAX's collectives and lax.ppermute only.
A program may use at most 192 MiB of HBM per device.

v0:
```python
import math

import jax
import jax.numpy as jnp
from jax import lax
from jax.sharding import Mesh, PartitionSpec as P

HEADS = 16
KV_HEADS = 8
HEAD = 96
EPS = 1e-05
THETA = 100000.0
f32 = jnp.float32
bf16 = jnp.bfloat16


def rope_tables(position_ids):
    half = HEAD // 2
    ladder = jnp.arange(half).astype(f32) * (2.0 / HEAD)
    inverse = jnp.exp(-math.log(THETA) * ladder)
    angles = position_ids.astype(f32)[:, None] * inverse[None, :]
    return jnp.cos(angles)[:, None, :], jnp.sin(angles)[:, None, :]


def rotate(vectors, cosine, sine):
    half = HEAD // 2
    a, b = vectors[..., :half], vectors[..., half:]
    return jnp.concatenate([a * cosine - b * sine, b * cosine + a * sine], axis=-1)


def unrotate(grads, cosine, sine):
    half = HEAD // 2
    a, b = grads[..., :half], grads[..., half:]
    return jnp.concatenate([a * cosine + b * sine, b * cosine - a * sine], axis=-1)


def rms_scale(values):
    return lax.rsqrt(jnp.mean(values * values, axis=-1, keepdims=True) + EPS)


def norm_back(grad, normed, scale):
    return scale * (grad - normed * jnp.mean(grad * normed, axis=-1, keepdims=True))


def mm(a, b):
    return jnp.dot(a, b, preferred_element_type=f32)


def mm_tn(a, b):
    return jnp.einsum("td,te->de", a, b, preferred_element_type=f32)


def mm_nt(a, b):
    return jnp.einsum("te,de->td", a, b, preferred_element_type=f32)


def on_device(
    block_input,
    positions,
    segments,
    out_cotangent,
    attn_gain,
    w_query,
    w_key,
    w_value,
    w_out,
    mlp_gain,
    w_gate,
    w_up,
    w_down,
):
    chips = lax.axis_size("chip")
    rows_z = lax.axis_size("fsdp")
    chip = lax.axis_index("chip")
    core = lax.axis_index("core")
    place = lax.axis_index("fsdp")
    tok = block_input.shape[2]
    width = block_input.shape[3]
    d_rows = w_query.shape[0]
    q_cols = w_query.shape[1] // chips
    kv_cols = w_key.shape[1] // chips
    ff_cols = w_gate.shape[1] // (2 * chips)
    kv_heads = KV_HEADS // chips
    factor = HEAD ** (-0.5)

    def core_swap(a):
        return lax.ppermute(a, "core", [(0, 1), (1, 0)])

    def chip_xor(a, j):
        return lax.ppermute(a, "chip", [(i, i ^ j) for i in range(chips)])

    def pick(a, index, axis=0):
        return lax.dynamic_index_in_dim(a, index, axis, keepdims=False)

    def gather_chips(a, axis=0):
        return jnp.concatenate([a] + [chip_xor(a, j) for j in range(1, chips)], axis=axis)

    def scatter_chips(a):
        step = a.shape[0] // chips
        total = a[:step]
        for j in range(1, chips):
            total = total + chip_xor(a[j * step : (j + 1) * step].astype(bf16), j).astype(f32)
        return total

    def by_chip(pieces):
        stacked = jnp.stack(pieces)
        bit = 1
        while bit < chips:
            view = stacked.reshape((chips // (2 * bit), 2, bit) + stacked.shape[1:])
            flipped = jnp.flip(view, axis=1)
            stacked = jnp.where((chip & bit) != 0, flipped, view).reshape(stacked.shape)
            bit *= 2
        return stacked

    def exchange_chips(pack):
        pieces = [pick(pack, chip)]
        for j in range(1, chips):
            pieces.append(chip_xor(pick(pack, chip ^ j), j))
        return by_chip(pieces)

    def core_pair(mine, other, axis):
        first = core == 0
        return jnp.stack([jnp.where(first, mine, other), jnp.where(first, other, mine)], axis)

    def both_cores(a):
        return core_pair(a, core_swap(a), 0)

    def chip_slices(weights, cols):
        return jnp.stack(
            [
                jnp.concatenate([w[:, k * n : (k + 1) * n] for w, n in zip(weights, cols)], axis=1)
                for k in range(chips)
            ]
        )

    def tie(*values):
        return lax.optimization_barrier(values)

    def along_z(a, step):
        return lax.ppermute(a, "fsdp", [(i, (i + step) % rows_z) for i in range(rows_z)])

    def ring_first(a):
        return along_z(a, 1), along_z(a, -1)

    def ring_rest(a, right, left):
        found = [(a, 0, 0), (right, -1, 0), (left, 1, 0)]
        for step in range(2, rows_z // 2 + 1):
            if 2 * step == rows_z:
                half = a.shape[-1] // 2
                found.append((along_z(right[..., :half], 1), -step, 0))
                found.append((along_z(left[..., half:], -1), step, half))
            else:
                right, left = along_z(right, 1), along_z(left, -1)
                found += [(right, -step, 0), (left, step, 0)]
        return found

    windows = [2 + (rows_z - 1) * w // 3 for w in range(4)]

    def part(a, index, start):
        index = lax.rem(index + 2 * rows_z, rows_z)
        size = (a.shape[0], 1, a.shape[2], a.shape[3] // 2)
        return lax.dynamic_slice(a, (0, index, 0, start), size)

    def scatter_begin(a):
        return part(a, place - 1, 0), part(a, place + 1, a.shape[3] // 2)

    def scatter_window(a, sums, window):
        low, high = sums
        for step in range(windows[window], windows[window + 1]):
            low = along_z(low, 1) + part(a, place - step, 0)
            high = along_z(high, -1) + part(a, place + step, a.shape[3] // 2)
        return low, high

    def assemble(found, groups):
        rows, cols = found[0][0].shape
        whole = jnp.zeros((groups, rows_z, rows // groups, cols), bf16)
        for piece, offset, column in found:
            piece = piece.reshape(groups, 1, rows // groups, piece.shape[-1])
            index = lax.rem(place + offset + rows_z, rows_z)
            whole = lax.dynamic_update_slice(whole, piece, (0, index, 0, column))
        return whole

    owner = (chip * 2 + core) * rows_z + place
    spot = chip * 2 + core
    spots = chips * 2
    gains = lax.dynamic_update_slice(
        jnp.zeros((2, width), f32),
        jnp.stack([attn_gain, mlp_gain]).astype(f32),
        (0, owner * d_rows),
    )
    marks = lax.dynamic_update_slice(
        jnp.zeros((4, spots * tok), f32),
        jnp.concatenate([positions[:, 0], segments[:, 0]]).astype(f32),
        (0, spot * tok),
    )
    table = jnp.concatenate([gains.reshape(-1), marks.reshape(-1)]).reshape(-1, 128)

    def sum_chips(a):
        bit = 1
        while bit < chips:
            a = a + chip_xor(a, bit)
            bit *= 2
        return a

    def sum_z(a, bit=1, end=rows_z):
        while bit < end:
            a = a + lax.ppermute(a, "fsdp", [(i, i ^ bit) for i in range(rows_z)])
            bit *= 2
        return a

    def again(found, pieces):
        return [(piece,) + f[1:] for piece, f in zip(pieces, found)]

    def pieces_of(found):
        return [f[0] for f in found]

    pack_qkv = chip_slices((w_query, w_key, w_value), (q_cols, kv_cols, kv_cols))
    piece_qkv = exchange_chips(pack_qkv).reshape(-1, pack_qkv.shape[-1])
    pair = jnp.stack([block_input[:, 0], out_cotangent[:, 0]], axis=1)
    pair = jnp.concatenate([pick(pair, core), core_swap(pick(pair, 1 - core))], axis=1)
    table = sum_chips(table + core_swap(table))
    rows = jnp.concatenate([w_out, w_down])
    rows = lax.all_gather(rows, "fsdp", axis=0)
    pack_gu = jnp.stack(
        [
            jnp.concatenate([w[:, n * ff_cols : (n + 1) * ff_cols] for w in (w_gate, w_up)], axis=1)
            for n in range(2 * chips)
        ]
    ).reshape(chips, 2, d_rows, 2 * ff_cols)
    pair, piece_qkv, table, pack_gu = tie(pair, piece_qkv, table, pack_gu)
    x_low, dy_low = pair[0], pair[1]

    qkv_right, qkv_left = ring_first(piece_qkv)
    piece_gu = exchange_chips(pack_gu)
    gains = sum_z(table.reshape(-1)[: 2 * width].reshape(2, width), 1, 2)
    qkv_right, qkv_left, piece_gu, x_low, gains = tie(qkv_right, qkv_left, piece_gu, x_low, gains)
    gains = sum_z(gains, 2, rows_z)

    near = [j for j in range(1, chips) if j & (j - 1) == 0]
    far = [j for j in range(1, chips) if j & (j - 1) != 0]
    x_parts = {0: x_low, **{j: chip_xor(x_low, j) for j in near}}
    found_qkv = ring_rest(piece_qkv, qkv_right, qkv_left)
    piece_gu = core_pair(pick(piece_gu, core, 1), core_swap(pick(piece_gu, 1 - core, 1)), 1)
    piece_gu = piece_gu.reshape(2 * chips * d_rows, 2 * ff_cols)
    order = sorted(x_parts)
    piece_gu, gains, *late = tie(piece_gu, gains, *[x_parts[j] for j in order], *pieces_of(found_qkv))
    x_parts = dict(zip(order, late))
    x_parts.update({j: chip_xor(x_parts[0], j) for j in far})
    x_all = jnp.concatenate([x_parts[j] for j in range(chips)])
    found_qkv = again(found_qkv, late[len(order) :])
    gu_right = along_z(piece_gu, 1)
    marks = pick(table.reshape(-1)[2 * width :].reshape(2, 2, spots, tok), core, 1)
    marks = jnp.concatenate(
        [pick(marks, (chip ^ k) * 2 + (core ^ c), 1) for k in range(chips) for c in range(2)],
        axis=1,
    )
    pos_all, seg_all = marks
    allowed = (seg_all[:, None] == seg_all[None, :]) & (pos_all[None, :] <= pos_all[:, None])
    cosine, sine = rope_tables(pos_all)
    w_qkv = assemble(found_qkv, chips)
    w_qkv = core_pair(w_qkv, core_swap(w_qkv), 1).reshape(width, -1)
    w_qkv, x_all, dy_low, cosine, sine, allowed, gu_right, piece_gu, rows = tie(
        w_qkv, x_all, dy_low, cosine, sine, allowed, gu_right, piece_gu, rows
    )
    along_out = rows[:, : w_out.shape[0]].reshape(-1, width)
    along_down = rows[:, w_out.shape[0] :].reshape(-1, width)
    gu_left = along_z(piece_gu, -1)
    gain_one, gain_two = gains
    own = x_low.shape[0]
    seq = x_all.shape[0]

    dy_all = gather_chips(dy_low)
    x_full = x_all.astype(f32)
    h_one = (x_full * rms_scale(x_full) * gain_one).astype(bf16)
    qkv = mm(h_one, w_qkv)
    q_rot = rotate(qkv[:, :q_cols].reshape(seq, kv_heads * 2, HEAD), cosine, sine)
    q_rot = q_rot.astype(bf16).reshape(seq, kv_heads, 2, HEAD)
    k_rot = rotate(
        qkv[:, q_cols : q_cols + kv_cols].reshape(seq, kv_heads, HEAD), cosine, sine
    ).astype(bf16)
    value = qkv[:, q_cols + kv_cols :].astype(bf16).reshape(seq, kv_heads, HEAD)
    out_w = both_cores(along_out).reshape(-1, width)
    scores = jnp.einsum("sgrh,tgh->grst", q_rot, k_rot, preferred_element_type=f32) * factor
    scores = jnp.where(allowed, scores, -1e30)
    raised = jnp.exp(scores - jnp.max(scores, axis=-1, keepdims=True))
    soft = raised / jnp.sum(raised, axis=-1, keepdims=True)
    soft_low = soft.astype(bf16)
    mixed = jnp.einsum("grst,tgh->sgrh", soft_low, value, preferred_element_type=f32)
    mixed = mixed.astype(bf16).reshape(seq, q_cols)
    mixed, dy_all, out_w, gu_left = tie(mixed, dy_all, out_w, gu_left)
    found_gu = ring_rest(piece_gu, gu_right, gu_left)
    x_own = x_low.astype(f32)
    middle = x_own + scatter_chips(mm(mixed, out_w))

    dy_both = jnp.concatenate([dy_all, core_swap(dy_all)])
    middle, dy_both, *late = tie(middle, dy_both, *pieces_of(found_gu))
    found_gu = again(found_gu, late)
    w_gu = assemble(found_gu, 2 * chips).reshape(width, 2 * ff_cols)
    scale_two = rms_scale(middle)
    n_two = middle * scale_two
    h_two = gather_chips((n_two * gain_two).astype(bf16))
    h_two, w_gu = tie(h_two, w_gu)
    h_both = jnp.concatenate([h_two, core_swap(h_two)])
    gu = mm(h_both, w_gu)
    gate, up = gu[:, :ff_cols], gu[:, ff_cols:]
    sigma = jax.nn.sigmoid(gate)
    act = (gate * sigma * up).astype(bf16)
    g_down = mm_tn(act, dy_both).astype(bf16)
    g_down, act = tie(g_down, act)
    g_down = lax.psum_scatter(g_down, "fsdp", scatter_dimension=0, tiled=True)
    d_act = mm_nt(dy_both, along_down)
    d_gate = (d_act * up * sigma * (1.0 + gate * (1.0 - sigma))).astype(bf16)
    d_up = (d_act * gate * sigma).astype(bf16)
    d_gu = jnp.concatenate([d_gate, d_up], axis=1)

    def give_partial(rows, weights, product):
        other = core_swap(product(rows[seq:], weights).astype(bf16)).astype(f32)
        return product(rows[:seq], weights) + other

    d_h_two = give_partial(d_gu, w_gu, mm_nt)
    g_gu = mm_tn(h_both, d_gu).astype(bf16).reshape(2 * chips, rows_z, d_rows, 2 * ff_cols)
    g_gu = jnp.transpose(g_gu, (1, 0, 2, 3)).reshape(width, 2 * ff_cols)
    d_h_two, g_gu = tie(scatter_chips(d_h_two), g_gu)
    g_gu = lax.psum_scatter(g_gu, "fsdp", scatter_dimension=0, tiled=True)

    dy_own = dy_low.astype(f32)
    gain_two_part = jnp.sum(d_h_two * n_two, axis=0)
    d_middle = dy_own + norm_back(d_h_two * gain_two, n_two, scale_two)
    branch = gather_chips(d_middle.astype(bf16))
    partial = give_partial(act, along_down, mm)
    branch, partial, g_down = tie(branch, partial, g_down)
    shares = {
        j: partial[j * own : (j + 1) * own].astype(bf16) if j else partial[:own]
        for j in range(chips)
    }
    shares.update({j: chip_xor(shares[j], j) for j in near})

    g_out = mm_tn(mixed, branch).astype(bf16)
    g_out = g_out.reshape(2, g_out.shape[0] // 2, g_out.shape[1])
    g_out = pick(g_out, core) + core_swap(pick(g_out, 1 - core))
    d_mixed = mm_nt(branch, out_w).astype(bf16).reshape(seq, kv_heads, 2, HEAD)
    d_soft = jnp.einsum("sgrh,tgh->grst", d_mixed, value, preferred_element_type=f32)
    d_value = jnp.einsum("grst,sgrh->tgh", soft_low, d_mixed, preferred_element_type=f32)
    inner = jnp.sum(soft * d_soft, axis=-1, keepdims=True)
    d_scores = (soft * (d_soft - inner)).astype(bf16)
    d_q = jnp.einsum("grst,tgh->sgrh", d_scores, k_rot, preferred_element_type=f32) * factor
    d_q, *late = tie(d_q, *[shares[j] for j in range(chips)])
    shares = dict(enumerate(late))
    shares.update({j: chip_xor(shares[j], j) for j in far})
    d_k = jnp.einsum("grst,sgrh->tgh", d_scores, q_rot, preferred_element_type=f32) * factor
    d_q = unrotate(d_q.reshape(seq, kv_heads * 2, HEAD), cosine, sine)
    d_k = unrotate(d_k, cosine, sine)
    d_qkv = jnp.concatenate(
        [
            d_q.reshape(seq, q_cols).astype(bf16),
            d_k.reshape(seq, kv_cols).astype(bf16),
            d_value.reshape(seq, kv_cols).astype(bf16),
        ],
        axis=1,
    )
    d_qkv, g_out = tie(d_qkv, g_out)
    cols_qkv = d_qkv.shape[1]
    g_qkv = mm_tn(h_one, d_qkv).astype(bf16).reshape(chips, 2, rows_z, d_rows, cols_qkv)
    g_qkv = pick(g_qkv, core, 1) + core_swap(pick(g_qkv, 1 - core, 1))
    g_qkv = jnp.transpose(g_qkv, (1, 0, 2, 3)).reshape(1, rows_z, chips * d_rows, cols_qkv)
    folds = width // cols_qkv
    g_out = g_out.reshape(1, rows_z, d_rows, width)
    g_rest = [g_out[..., k * cols_qkv : (k + 1) * cols_qkv] for k in range(folds)]
    g_rest = jnp.concatenate([g_qkv] + g_rest, axis=2)
    d_h_one = mm_nt(d_qkv, w_qkv)
    result = middle + shares[0]
    for j in range(1, chips):
        result = result + shares[j].astype(f32)
    g_rest, d_h_one, result = tie(g_rest, d_h_one, result.astype(bf16))
    sums = scatter_window(g_rest, scatter_begin(g_rest), 0)
    d_h_one, *sums = tie(scatter_chips(d_h_one), *sums)
    scale_one = rms_scale(x_own)
    n_one = x_own * scale_one
    gain_one_part = jnp.sum(d_h_one * n_one, axis=0)
    gain_parts = jnp.stack([gain_one_part, gain_two_part])
    gain_parts = sum_chips(gain_parts + core_swap(gain_parts))
    gain_parts, *sums = tie(gain_parts, *scatter_window(g_rest, sums, 1))
    sums = scatter_window(g_rest, sums, 2)
    g_rest = jnp.concatenate(sums, axis=-1).reshape(-1, cols_qkv)
    d_input = (d_middle + norm_back(d_h_one * gain_one, n_one, scale_one)).astype(bf16)

    def give_back(a):
        mine, theirs = a[:tok], core_swap(a[tok:])
        first = core == 0
        return jnp.stack([jnp.where(first, mine, theirs), jnp.where(first, theirs, mine)])[:, None]

    def spread(grad, start, cols):
        part = grad[:, :, start : start + cols].astype(f32)
        return jnp.transpose(part, (1, 0, 2)).reshape(d_rows, chips * cols)

    def spread_ff(grad):
        grad = jnp.transpose(grad.astype(f32), (2, 0, 1, 3))
        return grad.reshape(d_rows, 2 * chips * ff_cols)

    g_down = g_down.astype(f32)
    g_gu = g_gu.reshape(chips, 2, d_rows, 2 * ff_cols)
    g_gu = core_pair(pick(g_gu, core, 1), core_swap(pick(g_gu, 1 - core, 1)), 1)
    g_gu = exchange_chips(g_gu)
    g_gate, g_up = spread_ff(g_gu[..., :ff_cols]), spread_ff(g_gu[..., ff_cols:])
    gain_parts = sum_z(gain_parts)
    gain_parts = lax.dynamic_slice_in_dim(gain_parts, owner * d_rows, d_rows, 1)
    result, d_input = give_back(result), give_back(d_input)
    g_rest, g_gate, g_up, g_down, gain_parts, result, d_input = tie(
        g_rest, g_gate, g_up, g_down, gain_parts, result, d_input
    )
    g_qkv = exchange_chips(g_rest[: chips * d_rows].reshape(chips, d_rows, cols_qkv))
    g_out = g_rest[chips * d_rows :].reshape(folds, d_rows, cols_qkv)
    g_out = jnp.transpose(g_out, (1, 0, 2)).reshape(d_rows, width).astype(f32)
    return (
        result,
        d_input,
        gain_parts[0],
        spread(g_qkv, 0, q_cols),
        spread(g_qkv, q_cols, kv_cols),
        spread(g_qkv, q_cols + kv_cols, kv_cols),
        g_out,
        gain_parts[1],
        g_gate,
        g_up,
        g_down,
    )


def solution(mesh):
    ctx, fsdp = mesh.shape["ctx"], mesh.shape["fsdp"]
    split = Mesh(mesh.devices.reshape(ctx // 2, 2, fsdp), ("chip", "core", "fsdp"))
    ctx_axes = ("chip", "core")
    all_axes = ("chip", "core", "fsdp")
    tokens = P(None, "fsdp", ctx_axes, None)
    marks = P(None, "fsdp", ctx_axes)
    vector, matrix = P(all_axes), P(all_axes, None)
    return jax.shard_map(
        on_device,
        mesh=split,
        in_specs=(
            tokens, marks, marks, tokens, vector, matrix, matrix, matrix, matrix,
            vector, matrix, matrix, matrix,
        ),
        out_specs=(
            tokens, tokens, vector, matrix, matrix, matrix, matrix, vector,
            matrix, matrix, matrix,
        ),
        check_vma=False,
    )
```

profile of v0, /device:TPU:0, one launch (start us, length us, event | category | flops | bytes accessed | tf_op | source)
XLA Modules:
  0.0 380.0 jit_solution(10092635541459052525)
XLA Ops:
  11.0 3.9 %collective-permute-start.3 = (bf16[48,768]{1,0:T(8,128)(2,1)}, bf16[48,768]{1,0:T(8,128)(2,1)}, u32[]{:S(2)}, u32[]{:S(2)}) collective-permute-start(bf16[48,768]{1,0:T(8,128)(2,1)} %get-tuple-element.278), channel_id=1, source_target_pairs={{0,24},{8,16},{16,8},{24,0},{1,25},{9,17},{17,9},{25,1},{2,26},{10... | collective-permute-start | bytes 221192 | tf_op jit(solution)/shard_map/ppermute | solution.py:90
  32.8 3.8 collective-permute-start.8
  36.6 2.5 collective-permute-done.10
  39.7 11.1 %collective-permute-done.7 = bf16[192,768]{1,0:T(8,128)(2,1)S(1)} collective-permute-done((bf16[192,768]{1,0:T(8,128)(2,1)S(1)}, bf16[192,768]{1,0:T(8,128)(2,1)S(1)}, u32[]{:S(2)}, u32[]{:S(2)}) %collective-permute-start.7) | collective-permute-done | bytes 294944 | tf_op jit(solution)/shard_map/ppermute | solution.py:140
  50.8 10.8 %collective-permute-done.8 = bf16[192,768]{1,0:T(8,128)(2,1)S(1)} collective-permute-done((bf16[192,768]{1,0:T(8,128)(2,1)S(1)}, bf16[192,768]{1,0:T(8,128)(2,1)S(1)}, u32[]{:S(2)}, u32[]{:S(2)}) %collective-permute-start.8) | collective-permute-done | bytes 294944 | tf_op jit(solution)/shard_map/ppermute | solution.py:140
  65.3 2.6 collective-permute-start.14
  70.4 2.9 collective-permute-start.18
  74.4 5.4 %collective-permute-done.17 = bf16[192,384]{1,0:T(8,128)(2,1)S(1)} collective-permute-done((bf16[192,384]{1,0:T(8,128)(2,1)S(1)}, bf16[192,384]{1,0:T(8,128)(2,1)S(1)}, u32[]{:S(2)}, u32[]{:S(2)}) %collective-permute-start.17) | collective-permute-done | bytes 147488 | tf_op jit(solution)/shard_map/ppermute | solution.py:140
  79.8 3.3 collective-permute-done.18
  90.0 6.1 %collective-permute-done.20 = bf16[128,1536]{1,0:T(8,128)(2,1)S(1)} collective-permute-done((bf16[128,1536]{1,0:T(8,128)(2,1)S(1)}, bf16[128,1536]{1,0:T(8,128)(2,1)S(1)}, u32[]{:S(2)}, u32[]{:S(2)}) %collective-permute-start.20) | collective-permute-done | bytes 393248 | tf_op jit(solution)/shard_map/ppermute | solution.py:90
  100.4 9.5 %collective-permute-done.21 = bf16[384,1024]{1,0:T(8,128)(2,1)} collective-permute-done((bf16[384,1024]{1,0:T(8,128)(2,1)}, bf16[384,1024]{1,0:T(8,128)(2,1)}, u32[]{:S(2)}, u32[]{:S(2)}) %collective-permute-start.21) | collective-permute-done | bytes 786464 | tf_op jit(solution)/shard_map/ppermute | solution.py:140
  111.0 2.3 collective-permute-start.24
  113.7 3.1 fusion.48
  128.7 4.9 %fusion.98 = (f32[2,2,512]{2,1,0:T(2,128)S(1)}, f32[2,2,512,512]{2,3,1,0:T(8,128)}) fusion(pred[512,512]{0,1:T(8,128)(4,1)} %compare_and_fusion, bf16[512,2,2,48]{0,3,2,1:T(8,128)(2,1)} %bitcast.404, bf16[512,2,2,48]{0,3,2,1:T(8,128)(2,1)} %bitcast.402, bf16[512,2,48]{0,2,1:T(8,128)(2,1)} %get-tuple-element.252, bf16[512,2,48]{0,2,1:T(8,128)(2,1)S(1)} %get-tuple-element.251), kind=kOutput, calls=%fused_computation.284 | convolution fusion | flops 206701056 | bytes 5054464 | tf_op jit(solution)/shard_map/sub | solution.py:285
  133.7 2.8 convolution_convert_fusion.6
  139.5 9.4 %collective-permute-done.26 = bf16[384,1024]{1,0:T(8,128)(2,1)S(1)} collective-permute-done((bf16[384,1024]{1,0:T(8,128)(2,1)}, bf16[384,1024]{1,0:T(8,128)(2,1)S(1)}, u32[]{:S(2)}, u32[]{:S(2)}) %collective-permute-start.26) | collective-permute-done | bytes 786464 | tf_op jit(solution)/shard_map/ppermute | solution.py:140
  151.2 2.3 collective-permute-start.29
  154.7 7.4 %collective-permute-done.27 = bf16[128,1536]{1,0:T(8,128)(2,1)S(1)} collective-permute-done((bf16[128,1536]{1,0:T(8,128)(2,1)S(1)}, bf16[128,1536]{1,0:T(8,128)(2,1)S(1)}, u32[]{:S(2)}, u32[]{:S(2)}) %collective-permute-start.27) | collective-permute-done | bytes 393248 | tf_op jit(solution)/shard_map/ppermute | solution.py:90
  164.2 6.2 %collective-permute-done.28 = bf16[128,1536]{1,0:T(8,128)(2,1)S(1)} collective-permute-done((bf16[128,1536]{1,0:T(8,128)(2,1)S(1)}, bf16[128,1536]{1,0:T(8,128)(2,1)S(1)}, u32[]{:S(2)}, u32[]{:S(2)}) %collective-permute-start.28) | collective-permute-done | bytes 393248 | tf_op jit(solution)/shard_map/ppermute | solution.py:90
  171.0 4.6 %collective-permute-done.32 = bf16[384,512]{1,0:T(8,128)(2,1)S(1)} collective-permute-done((bf16[384,512]{1,0:T(8,128)(2,1)S(1)}, bf16[384,512]{1,0:T(8,128)(2,1)S(1)}, u32[]{:S(2)}, u32[]{:S(2)}) %collective-permute-start.32) | collective-permute-done | bytes 393248 | tf_op jit(solution)/shard_map/ppermute | solution.py:140
  177.1 2.4 collective-permute-start.35
  182.5 5.5 %collective-permute-done.33 = bf16[128,1536]{1,0:T(8,128)(2,1)S(1)} collective-permute-done((bf16[128,1536]{1,0:T(8,128)(2,1)S(1)}, bf16[128,1536]{1,0:T(8,128)(2,1)S(1)}, u32[]{:S(2)}, u32[]{:S(2)}) %collective-permute-start.33) | collective-permute-done | bytes 393248 | tf_op jit(solution)/shard_map/ppermute | solution.py:90
  188.0 7.8 %collective-permute-done.34 = bf16[128,1536]{1,0:T(8,128)(2,1)S(1)} collective-permute-done((bf16[128,1536]{1,0:T(8,128)(2,1)S(1)}, bf16[128,1536]{1,0:T(8,128)(2,1)S(1)}, u32[]{:S(2)}, u32[]{:S(2)}) %collective-permute-start.34) | collective-permute-done | bytes 393248 | tf_op jit(solution)/shard_map/ppermute | solution.py:90
  196.2 3.2 collective-permute-done.36
  199.4 3.6 fusion.101
  203.0 3.5 multiply_convert_fusion.1
  206.6 3.0 convolution_convert_fusion.4
  210.3 5.2 %convolution_convert_fusion.3 = bf16[512,1536]{1,0:T(8,128)(2,1)} fusion(bf16[1024,512]{0,1:T(8,128)(2,1)} %get-tuple-element.124, bf16[1024,1536]{1,0:T(8,128)(2,1)} %copy-done.8), kind=kOutput, calls=%fused_computation.20 | convolution fusion | flops 1611399168 | bytes 5767168 | tf_op jit(solution)/shard_map/td,te->de/dot_general | solution.py:50
  215.5 3.7 convolution_convert_fusion.2
  219.8 4.7 %fusion.100 = (bf16[512,1536]{1,0:T(8,128)(2,1)S(1)}, f32[512,1536]{1,0:T(8,128)S(1)}) fusion(bf16[512,1536]{1,0:T(8,128)(2,1)} %collective-permute-done.37, bf16[1536,1024]{1,0:T(8,128)(2,1)} %bitcast.361, bf16[1024,512]{0,1:T(8,128)(2,1)} %copy-done.56, bf16[1024,512]{0,1:T(8,128)(2,1)} %copy-done.54), kind=kOutput, calls=%fused_computation.286 | convolution fusion | flops 1615069184 | bytes 11534336 | tf_op jit(solution)/shard_map/te,de->td/dot_general | solution.py:54
  228.2 4.7 %convolution_convert_fusion = bf16[1536,1024]{1,0:T(8,128)(2,1)S(1)} fusion(bf16[1024,1536]{1,0:T(8,128)(2,1)S(1)} %copy-done.19, bf16[1024,512]{0,1:T(8,128)(2,1)S(1)} %copy-done.55, bf16[1024,512]{0,1:T(8,128)(2,1)S(1)} %copy-done.57), kind=kOutput, calls=%fused_computation.10 | convolution fusion | flops 3226992640 | bytes 8388608 | tf_op jit(solution)/shard_map/td,te->de/dot_general | solution.py:50
  236.6 8.8 %collective-permute-done.39 = bf16[128,1536]{1,0:T(8,128)(2,1)S(1)} collective-permute-done((bf16[128,1536]{1,0:T(8,128)(2,1)S(1)}, bf16[128,1536]{1,0:T(8,128)(2,1)S(1)}, u32[]{:S(2)}, u32[]{:S(2)}) %collective-permute-start.39) | collective-permute-done | bytes 393248 | tf_op jit(solution)/shard_map/ppermute | solution.py:90
  251.6 4.1 %convert_add_fusion = f32[512,1536]{1,0:T(8,128)} fusion(bf16[512,1536]{1,0:T(8,128)(2,1)} %collective-permute-done.44, bf16[512,1536]{1,0:T(8,128)(2,1)S(1)} %bitcast.350, bf16[1024,512]{0,1:T(8,128)(2,1)S(1)} %copy-done.25), kind=kOutput, calls=%fused_computation.17 | convolution fusion | flops 806879232 | bytes 6815744 | tf_op jit(solution)/shard_map/dot_general | solution.py:46
  255.8 4.6 %collective-permute-done.41 = bf16[128,1536]{1,0:T(8,128)(2,1)} collective-permute-done((bf16[128,1536]{1,0:T(8,128)(2,1)}, bf16[128,1536]{1,0:T(8,128)(2,1)}, u32[]{:S(2)}, u32[]{:S(2)}) %collective-permute-start.41) | collective-permute-done | bytes 393248 | tf_op jit(solution)/shard_map/ppermute | solution.py:90
  260.4 6.7 %collective-permute-done.42 = bf16[128,1536]{1,0:T(8,128)(2,1)} collective-permute-done((bf16[128,1536]{1,0:T(8,128)(2,1)}, bf16[128,1536]{1,0:T(8,128)(2,1)}, u32[]{:S(2)}, u32[]{:S(2)}) %collective-permute-start.42) | collective-permute-done | bytes 393248 | tf_op jit(solution)/shard_map/ppermute | solution.py:90
  267.2 2.7 pad_maximum_fusion.8
  283.5 3.0 collective-permute-done.45
  294.5 2.4 collective-permute-done.49
  298.3 3.2 collective-permute-start.54
  305.5 6.9 %collective-permute-done.53 = bf16[1,1,288,384]{3,2,1,0:T(8,128)(2,1)S(1)} collective-permute-done((bf16[1,1,288,384]{3,2,1,0:T(8,128)(2,1)S(1)}, bf16[1,1,288,384]{3,2,1,0:T(8,128)(2,1)S(1)}, u32[]{:S(2)}, u32[]{:S(2)}) %collective-permute-start.53) | collective-permute-done | bytes 221216 | tf_op jit(solution)/shard_map/ppermute | solution.py:140
  312.4 7.0 %collective-permute-done.54 = bf16[1,1,288,384]{3,2,1,0:T(8,128)(2,1)S(1)} collective-permute-done((bf16[1,1,288,384]{3,2,1,0:T(8,128)(2,1)S(1)}, bf16[1,1,288,384]{3,2,1,0:T(8,128)(2,1)S(1)}, u32[]{:S(2)}, u32[]{:S(2)}) %collective-permute-start.54) | collective-permute-done | bytes 221216 | tf_op jit(solution)/shard_map/ppermute | solution.py:140
  319.5 2.7 collective-permute-done.51
  325.6 3.8 %collective-permute-start.59 = (bf16[1,1,288,384]{3,2,1,0:T(8,128)(2,1)S(1)}, bf16[1,1,288,384]{3,2,1,0:T(8,128)(2,1)S(1)}, u32[]{:S(2)}, u32[]{:S(2)}) collective-permute-start(bf16[1,1,288,384]{3,2,1,0:T(8,128)(2,1)S(1)} %get-tuple-element.139), channel_id=1, source_target_pairs={{0,3},{1,0},{2,1},{3,2},{4,7},{5,4},{6,5},{7,6},{8,11},{9,8},{10,9... | collective-permute-start | bytes 663560 | tf_op jit(solution)/shard_map/ppermute | solution.py:140
  330.5 2.7 collective-permute-done.57
  333.2 2.5 collective-permute-done.58
  339.0 2.4 collective-permute-done.66
  341.4 2.5 collective-permute-start.67
  344.9 3.6 collective-permute-start.61
  (425 shorter events, 142.3 us)
Async XLA Ops:
  7.2 102.6 %all-gather.3.cloned.1.call-start = ((), (), s32[]{:S(2)}) async-start(), calls=%async_computation.4 | async-start | bytes 2703360 | tf_op jit(solution)/shard_map/all_gather | solution.py:223
  11.0 14.6 %collective-permute-start.3 = (bf16[48,768]{1,0:T(8,128)(2,1)}, bf16[48,768]{1,0:T(8,128)(2,1)}, u32[]{:S(2)}, u32[]{:S(2)}) collective-permute-start(bf16[48,768]{1,0:T(8,128)(2,1)} %get-tuple-element.278), channel_id=1, source_target_pairs={{0,24},{8,16},{16,8},{24,0},{1,25},{9,17},{17,9},{25,1},{2,26},{10... | collective-permute-start | bytes 221192 | tf_op jit(solution)/shard_map/ppermute | solution.py:90
  14.9 10.6 %collective-permute-start.1 = (bf16[48,768]{1,0:T(8,128)(2,1)}, bf16[48,768]{1,0:T(8,128)(2,1)}, u32[]{:S(2)}, u32[]{:S(2)}) collective-permute-start(bf16[48,768]{1,0:T(8,128)(2,1)} %get-tuple-element.280), channel_id=1, source_target_pairs={{0,8},{8,0},{16,24},{24,16},{1,9},{9,1},{17,25},{25,17},{2,10},{10... | collective-permute-start | bytes 221192 | tf_op jit(solution)/shard_map/ppermute | solution.py:90
  15.5 10.1 %collective-permute-start.2 = (bf16[48,768]{1,0:T(8,128)(2,1)S(1)}, bf16[48,768]{1,0:T(8,128)(2,1)}, u32[]{:S(2)}, u32[]{:S(2)}) collective-permute-start(bf16[48,768]{1,0:T(8,128)(2,1)S(1)} %get-tuple-element.279), channel_id=1, source_target_pairs={{0,16},{8,24},{16,0},{24,8},{1,17},{9,25},{17,1},{25,9},{2,18},{10... | collective-permute-start | bytes 221192 | tf_op jit(solution)/shard_map/ppermute | solution.py:90
  16.2 10.5 %collective-permute-start = (bf16[2,64,1536]{2,1,0:T(8,128)(2,1)S(1)}, bf16[2,64,1536]{2,1,0:T(8,128)(2,1)S(1)}, u32[]{:S(2)}, u32[]{:S(2)}) collective-permute-start(bf16[2,64,1536]{2,1,0:T(8,128)(2,1)S(1)} %get-tuple-element.242), channel_id=1, source_target_pairs={{0,4},{4,0},{1,5},{5,1},{2,6},{6,2},{3,7},{7,3},{8,12},{12,8},{9,1... | collective-permute-start | bytes 1179656 | tf_op jit(solution)/shard_map/ppermute | solution.py:87
  17.6 252.2 %reduce-scatter.3.cloned.1.call-start = ((), (), s32[]{:S(2)}) async-start(), calls=%async_computation.2 | async-start | bytes 1966080 | tf_op jit(solution)/shard_map/reduce_scatter | solution.py:310
  32.7 18.1 %collective-permute-start.7 = (bf16[192,768]{1,0:T(8,128)(2,1)S(1)}, bf16[192,768]{1,0:T(8,128)(2,1)S(1)}, u32[]{:S(2)}, u32[]{:S(2)}) collective-permute-start(bf16[192,768]{1,0:T(8,128)(2,1)S(1)} %bitcast.393), channel_id=1, source_target_pairs={{0,1},{1,2},{2,3},{3,0},{4,5},{5,6},{6,7},{7,4},{8,9},{9,10},{10,1... | collective-permute-start | bytes 884744 | tf_op jit(solution)/shard_map/ppermute | solution.py:140
  32.8 28.8 %collective-permute-start.8 = (bf16[192,768]{1,0:T(8,128)(2,1)S(1)}, bf16[192,768]{1,0:T(8,128)(2,1)S(1)}, u32[]{:S(2)}, u32[]{:S(2)}) collective-permute-start(bf16[192,768]{1,0:T(8,128)(2,1)S(1)} %bitcast.394), channel_id=1, source_target_pairs={{0,3},{1,0},{2,1},{3,2},{4,7},{5,4},{6,5},{7,6},{8,11},{9,8},{10,9... | collective-permute-start | bytes 884744 | tf_op jit(solution)/shard_map/ppermute | solution.py:140
  61.6 11.7 %collective-permute-start.13 = (bf16[4,48,1024]{2,1,0:T(8,128)(2,1)S(1)}, bf16[4,48,1024]{2,1,0:T(8,128)(2,1)S(1)}, u32[]{:S(2)}, u32[]{:S(2)}) collective-permute-start(bf16[4,48,1024]{2,1,0:T(8,128)(2,1)S(1)} %dynamic-slice_bitcast_fusion.2), channel_id=1, source_target_pairs={{0,4},{4,0},{1,5},{5,1},{2,6},{6,2},{3,7},{7,3},{8,12},{12,8},{9,1... | collective-permute-start | bytes 1179656 | tf_op jit(solution)/shard_map/ppermute | solution.py:87
  62.3 20.8 %collective-permute-start.15 = (bf16[128,1536]{1,0:T(8,128)(2,1)S(1)}, bf16[128,1536]{1,0:T(8,128)(2,1)}, u32[]{:S(2)}, u32[]{:S(2)}) collective-permute-start(bf16[128,1536]{1,0:T(8,128)(2,1)S(1)} %get-tuple-element.96), channel_id=1, source_target_pairs={{0,8},{8,0},{16,24},{24,16},{1,9},{9,1},{17,25},{25,17},{2,10},{10... | collective-permute-start | bytes 1179656 | tf_op jit(solution)/shard_map/ppermute | solution.py:90
  63.8 19.3 %collective-permute-start.16 = (bf16[128,1536]{1,0:T(8,128)(2,1)S(1)}, bf16[128,1536]{1,0:T(8,128)(2,1)}, u32[]{:S(2)}, u32[]{:S(2)}) collective-permute-start(bf16[128,1536]{1,0:T(8,128)(2,1)S(1)} %get-tuple-element.96), channel_id=1, source_target_pairs={{0,16},{8,24},{16,0},{24,8},{1,17},{9,25},{17,1},{25,9},{2,18},{10... | collective-permute-start | bytes 1179656 | tf_op jit(solution)/shard_map/ppermute | solution.py:90
  68.1 11.7 %collective-permute-start.17 = (bf16[192,384]{1,0:T(8,128)(2,1)S(1)}, bf16[192,384]{1,0:T(8,128)(2,1)S(1)}, u32[]{:S(2)}, u32[]{:S(2)}) collective-permute-start(bf16[192,384]{1,0:T(8,128)(2,1)S(1)} %slice.303), channel_id=1, source_target_pairs={{0,1},{1,2},{2,3},{3,0},{4,5},{5,6},{6,7},{7,4},{8,9},{9,10},{10,1... | collective-permute-start | bytes 442376 | tf_op jit(solution)/shard_map/ppermute | solution.py:140
  70.4 12.7 %collective-permute-start.18 = (bf16[192,384]{1,0:T(8,128)(2,1)S(1)}, bf16[192,384]{1,0:T(8,128)(2,1)S(1)}, u32[]{:S(2)}, u32[]{:S(2)}) collective-permute-start(bf16[192,384]{1,0:T(8,128)(2,1)S(1)} %slice.304), channel_id=1, source_target_pairs={{0,3},{1,0},{2,1},{3,2},{4,7},{5,4},{6,5},{7,6},{8,11},{9,8},{10,9... | collective-permute-start | bytes 442376 | tf_op jit(solution)/shard_map/ppermute | solution.py:140
  83.4 13.9 %collective-permute-start.19 = (bf16[4,4,48,768]{3,2,1,0:T(8,128)(2,1)S(1)}, bf16[4,4,48,768]{3,2,1,0:T(8,128)(2,1)}, u32[]{:S(2)}, u32[]{:S(2)}) collective-permute-start(bf16[4,4,48,768]{3,2,1,0:T(8,128)(2,1)S(1)} %constant_dynamic-update-slice_fusion.9), channel_id=1, source_target_pairs={{0,4},{4,0},{1,5},{5,1},{2,6},{6,2},{3,7},{7,3},{8,12},{12,8},{9,1... | collective-permute-start | bytes 3538952 | tf_op jit(solution)/shard_map/ppermute | solution.py:87
  83.7 12.3 %collective-permute-start.20 = (bf16[128,1536]{1,0:T(8,128)(2,1)S(1)}, bf16[128,1536]{1,0:T(8,128)(2,1)S(1)}, u32[]{:S(2)}, u32[]{:S(2)}) collective-permute-start(bf16[128,1536]{1,0:T(8,128)(2,1)S(1)} %get-tuple-element.96), channel_id=1, source_target_pairs={{0,24},{8,16},{16,8},{24,0},{1,25},{9,17},{17,9},{25,1},{2,26},{10... | collective-permute-start | bytes 1179656 | tf_op jit(solution)/shard_map/ppermute | solution.py:90
  88.1 21.8 %collective-permute-start.21 = (bf16[384,1024]{1,0:T(8,128)(2,1)}, bf16[384,1024]{1,0:T(8,128)(2,1)}, u32[]{:S(2)}, u32[]{:S(2)}) collective-permute-start(bf16[384,1024]{1,0:T(8,128)(2,1)} %bitcast.43), channel_id=1, source_target_pairs={{0,1},{1,2},{2,3},{3,0},{4,5},{5,6},{6,7},{7,4},{8,9},{9,10},{10,1... | collective-permute-start | bytes 2359304 | tf_op jit(solution)/shard_map/ppermute | solution.py:140
  109.8 26.7 %collective-permute-start.22 = (bf16[128,1536]{1,0:T(8,128)(2,1)S(1)}, bf16[128,1536]{1,0:T(8,128)(2,1)}, u32[]{:S(2)}, u32[]{:S(2)}) collective-permute-start(bf16[128,1536]{1,0:T(8,128)(2,1)S(1)} %get-tuple-element.106), channel_id=1, source_target_pairs={{0,8},{8,0},{16,24},{24,16},{1,9},{9,1},{17,25},{25,17},{2,10},{10... | collective-permute-start | bytes 1179656 | tf_op jit(solution)/shard_map/ppermute | solution.py:90
  110.5 26.1 %collective-permute-start.23 = (bf16[128,1536]{1,0:T(8,128)(2,1)S(1)}, bf16[128,1536]{1,0:T(8,128)(2,1)}, u32[]{:S(2)}, u32[]{:S(2)}) collective-permute-start(bf16[128,1536]{1,0:T(8,128)(2,1)S(1)} %get-tuple-element.106), channel_id=1, source_target_pairs={{0,16},{8,24},{16,0},{24,8},{1,17},{9,25},{17,1},{25,9},{2,18},{10... | collective-permute-start | bytes 1179656 | tf_op jit(solution)/shard_map/ppermute | solution.py:90
  111.0 25.5 %collective-permute-start.24 = (bf16[128,1536]{1,0:T(8,128)(2,1)S(1)}, bf16[128,1536]{1,0:T(8,128)(2,1)}, u32[]{:S(2)}, u32[]{:S(2)}) collective-permute-start(bf16[128,1536]{1,0:T(8,128)(2,1)S(1)} %get-tuple-element.106), channel_id=1, source_target_pairs={{0,24},{8,16},{16,8},{24,0},{1,25},{9,17},{17,9},{25,1},{2,26},{10... | collective-permute-start | bytes 1179656 | tf_op jit(solution)/shard_map/ppermute | solution.py:90
  120.5 17.5 %collective-permute-start.25 = (bf16[192,1536]{1,0:T(8,128)(2,1)}, bf16[192,1536]{1,0:T(8,128)(2,1)}, u32[]{:S(2)}, u32[]{:S(2)}) collective-permute-start(bf16[192,1536]{1,0:T(8,128)(2,1)} %bitcast.82), channel_id=1, source_target_pairs={{0,4},{4,0},{1,5},{5,1},{2,6},{6,2},{3,7},{7,3},{8,12},{12,8},{9,1... | collective-permute-start | bytes 1769480 | tf_op jit(solution)/shard_map/ppermute | solution.py:87
  128.3 20.6 %collective-permute-start.26 = (bf16[384,1024]{1,0:T(8,128)(2,1)}, bf16[384,1024]{1,0:T(8,128)(2,1)S(1)}, u32[]{:S(2)}, u32[]{:S(2)}) collective-permute-start(bf16[384,1024]{1,0:T(8,128)(2,1)} %bitcast.43), channel_id=1, source_target_pairs={{0,3},{1,0},{2,1},{3,2},{4,7},{5,4},{6,5},{7,6},{8,11},{9,8},{10,9... | collective-permute-start | bytes 2359304 | tf_op jit(solution)/shard_map/ppermute | solution.py:140
  148.9 21.9 %collective-permute-start.30 = (bf16[512,1536]{1,0:T(8,128)(2,1)S(1)}, bf16[512,1536]{1,0:T(8,128)(2,1)S(1)}, u32[]{:S(2)}, u32[]{:S(2)}) collective-permute-start(bf16[512,1536]{1,0:T(8,128)(2,1)S(1)} %pad_maximum_fusion.6), channel_id=1, source_target_pairs={{0,4},{4,0},{1,5},{5,1},{2,6},{6,2},{3,7},{7,3},{8,12},{12,8},{9,1... | collective-permute-start | bytes 4718600 | tf_op jit(solution)/shard_map/ppermute | solution.py:87
  150.0 12.1 %collective-permute-start.27 = (bf16[128,1536]{1,0:T(8,128)(2,1)S(1)}, bf16[128,1536]{1,0:T(8,128)(2,1)S(1)}, u32[]{:S(2)}, u32[]{:S(2)}) collective-permute-start(bf16[128,1536]{1,0:T(8,128)(2,1)S(1)} %get-tuple-element.216), channel_id=1, source_target_pairs={{0,8},{8,0},{16,24},{24,16},{1,9},{9,1},{17,25},{25,17},{2,10},{10... | collective-permute-start | bytes 1179656 | tf_op jit(solution)/shard_map/ppermute | solution.py:90
  150.7 19.7 %collective-permute-start.28 = (bf16[128,1536]{1,0:T(8,128)(2,1)S(1)}, bf16[128,1536]{1,0:T(8,128)(2,1)S(1)}, u32[]{:S(2)}, u32[]{:S(2)}) collective-permute-start(bf16[128,1536]{1,0:T(8,128)(2,1)S(1)} %get-tuple-element.218), channel_id=1, source_target_pairs={{0,16},{8,24},{16,0},{24,8},{1,17},{9,25},{17,1},{25,9},{2,18},{10... | collective-permute-start | bytes 1179656 | tf_op jit(solution)/shard_map/ppermute | solution.py:90
  151.2 19.1 %collective-permute-start.29 = (bf16[128,1536]{1,0:T(8,128)(2,1)S(1)}, bf16[128,1536]{1,0:T(8,128)(2,1)S(1)}, u32[]{:S(2)}, u32[]{:S(2)}) collective-permute-start(bf16[128,1536]{1,0:T(8,128)(2,1)S(1)} %get-tuple-element.217), channel_id=1, source_target_pairs={{0,24},{8,16},{16,8},{24,0},{1,25},{9,17},{17,9},{25,1},{2,26},{10... | collective-permute-start | bytes 1179656 | tf_op jit(solution)/shard_map/ppermute | solution.py:90
  154.6 16.4 %collective-permute-start.31 = (bf16[384,512]{1,0:T(8,128)(2,1)S(1)}, bf16[384,512]{1,0:T(8,128)(2,1)S(1)}, u32[]{:S(2)}, u32[]{:S(2)}) collective-permute-start(bf16[384,512]{1,0:T(8,128)(2,1)S(1)} %slice.319), channel_id=1, source_target_pairs={{0,1},{1,2},{2,3},{3,0},{4,5},{5,6},{6,7},{7,4},{8,9},{9,10},{10,1... | collective-permute-start | bytes 1179656 | tf_op jit(solution)/shard_map/ppermute | solution.py:140
  162.1 13.5 %collective-permute-start.32 = (bf16[384,512]{1,0:T(8,128)(2,1)S(1)}, bf16[384,512]{1,0:T(8,128)(2,1)S(1)}, u32[]{:S(2)}, u32[]{:S(2)}) collective-permute-start(bf16[384,512]{1,0:T(8,128)(2,1)S(1)} %slice.320), channel_id=1, source_target_pairs={{0,3},{1,0},{2,1},{3,2},{4,7},{5,4},{6,5},{7,6},{8,11},{9,8},{10,9... | collective-permute-start | bytes 1179656 | tf_op jit(solution)/shard_map/ppermute | solution.py:140
  175.9 12.1 %collective-permute-start.33 = (bf16[128,1536]{1,0:T(8,128)(2,1)S(1)}, bf16[128,1536]{1,0:T(8,128)(2,1)S(1)}, u32[]{:S(2)}, u32[]{:S(2)}) collective-permute-start(bf16[128,1536]{1,0:T(8,128)(2,1)S(1)} %multiply_convert_fusion.3), channel_id=1, source_target_pairs={{0,8},{8,0},{16,24},{24,16},{1,9},{9,1},{17,25},{25,17},{2,10},{10... | collective-permute-start | bytes 1179656 | tf_op jit(solution)/shard_map/ppermute | solution.py:90
  176.5 19.2 %collective-permute-start.34 = (bf16[128,1536]{1,0:T(8,128)(2,1)S(1)}, bf16[128,1536]{1,0:T(8,128)(2,1)S(1)}, u32[]{:S(2)}, u32[]{:S(2)}) collective-permute-start(bf16[128,1536]{1,0:T(8,128)(2,1)S(1)} %multiply_convert_fusion.3), channel_id=1, source_target_pairs={{0,16},{8,24},{16,0},{24,8},{1,17},{9,25},{17,1},{25,9},{2,18},{10... | collective-permute-start | bytes 1179656 | tf_op jit(solution)/shard_map/ppermute | solution.py:90
  177.1 18.6 %collective-permute-start.35 = (bf16[128,1536]{1,0:T(8,128)(2,1)S(1)}, bf16[128,1536]{1,0:T(8,128)(2,1)S(1)}, u32[]{:S(2)}, u32[]{:S(2)}) collective-permute-start(bf16[128,1536]{1,0:T(8,128)(2,1)S(1)} %multiply_convert_fusion.3), channel_id=1, source_target_pairs={{0,24},{8,16},{16,8},{24,0},{1,25},{9,17},{17,9},{25,1},{2,26},{10... | collective-permute-start | bytes 1179656 | tf_op jit(solution)/shard_map/ppermute | solution.py:90
  209.6 10.2 %collective-permute-start.37 = (bf16[512,1536]{1,0:T(8,128)(2,1)}, bf16[512,1536]{1,0:T(8,128)(2,1)}, u32[]{:S(2)}, u32[]{:S(2)}) collective-permute-start(bf16[512,1536]{1,0:T(8,128)(2,1)} %convolution_convert_fusion.4), channel_id=1, source_target_pairs={{0,4},{4,0},{1,5},{5,1},{2,6},{6,2},{3,7},{7,3},{8,12},{12,8},{9,1... | collective-permute-start | bytes 4718600 | tf_op jit(solution)/shard_map/ppermute | solution.py:87
  219.2 32.4 %collective-permute-start.44 = (bf16[512,1536]{1,0:T(8,128)(2,1)}, bf16[512,1536]{1,0:T(8,128)(2,1)}, u32[]{:S(2)}, u32[]{:S(2)}) collective-permute-start(bf16[512,1536]{1,0:T(8,128)(2,1)} %convolution_convert_fusion.2), channel_id=1, source_target_pairs={{0,4},{4,0},{1,5},{5,1},{2,6},{6,2},{3,7},{7,3},{8,12},{12,8},{9,1... | collective-permute-start | bytes 4718600 | tf_op jit(solution)/shard_map/ppermute | solution.py:87
  219.6 118.1 %reduce-scatter.5.cloned.1.call-start = ((), (), s32[]{:S(2)}) async-start(), calls=%async_computation.3 | async-start | bytes 3932160 | tf_op jit(solution)/shard_map/reduce_scatter | solution.py:324
  224.6 12.1 %collective-permute-start.38 = (bf16[128,1536]{1,0:T(8,128)(2,1)S(1)}, bf16[128,1536]{1,0:T(8,128)(2,1)S(1)}, u32[]{:S(2)}, u32[]{:S(2)}) collective-permute-start(bf16[128,1536]{1,0:T(8,128)(2,1)S(1)} %get-tuple-element.213), channel_id=1, source_target_pairs={{0,8},{8,0},{16,24},{24,16},{1,9},{9,1},{17,25},{25,17},{2,10},{10... | collective-permute-start | bytes 1179656 | tf_op jit(solution)/shard_map/ppermute | solution.py:90
  226.1 19.3 %collective-permute-start.39 = (bf16[128,1536]{1,0:T(8,128)(2,1)S(1)}, bf16[128,1536]{1,0:T(8,128)(2,1)S(1)}, u32[]{:S(2)}, u32[]{:S(2)}) collective-permute-start(bf16[128,1536]{1,0:T(8,128)(2,1)S(1)} %get-tuple-element.215), channel_id=1, source_target_pairs={{0,16},{8,24},{16,0},{24,8},{1,17},{9,25},{17,1},{25,9},{2,18},{10... | collective-permute-start | bytes 1179656 | tf_op jit(solution)/shard_map/ppermute | solution.py:90
  226.7 18.8 %collective-permute-start.40 = (bf16[128,1536]{1,0:T(8,128)(2,1)S(1)}, bf16[128,1536]{1,0:T(8,128)(2,1)S(1)}, u32[]{:S(2)}, u32[]{:S(2)}) collective-permute-start(bf16[128,1536]{1,0:T(8,128)(2,1)S(1)} %get-tuple-element.214), channel_id=1, source_target_pairs={{0,24},{8,16},{16,8},{24,0},{1,25},{9,17},{17,9},{25,1},{2,26},{10... | collective-permute-start | bytes 1179656 | tf_op jit(solution)/shard_map/ppermute | solution.py:90
  248.1 12.3 %collective-permute-start.41 = (bf16[128,1536]{1,0:T(8,128)(2,1)}, bf16[128,1536]{1,0:T(8,128)(2,1)}, u32[]{:S(2)}, u32[]{:S(2)}) collective-permute-start(bf16[128,1536]{1,0:T(8,128)(2,1)} %fusion.86), channel_id=1, source_target_pairs={{0,8},{8,0},{16,24},{24,16},{1,9},{9,1},{17,25},{25,17},{2,10},{10... | collective-permute-start | bytes 1179656 | tf_op jit(solution)/shard_map/ppermute | solution.py:90
  248.7 18.5 %collective-permute-start.42 = (bf16[128,1536]{1,0:T(8,128)(2,1)}, bf16[128,1536]{1,0:T(8,128)(2,1)}, u32[]{:S(2)}, u32[]{:S(2)}) collective-permute-start(bf16[128,1536]{1,0:T(8,128)(2,1)} %fusion.86), channel_id=1, source_target_pairs={{0,16},{8,24},{16,0},{24,8},{1,17},{9,25},{17,1},{25,9},{2,18},{10... | collective-permute-start | bytes 1179656 | tf_op jit(solution)/shard_map/ppermute | solution.py:90
  249.8 17.3 %collective-permute-start.43 = (bf16[128,1536]{1,0:T(8,128)(2,1)}, bf16[128,1536]{1,0:T(8,128)(2,1)}, u32[]{:S(2)}, u32[]{:S(2)}) collective-permute-start(bf16[128,1536]{1,0:T(8,128)(2,1)} %fusion.86), channel_id=1, source_target_pairs={{0,24},{8,16},{16,8},{24,0},{1,25},{9,17},{17,9},{25,1},{2,26},{10... | collective-permute-start | bytes 1179656 | tf_op jit(solution)/shard_map/ppermute | solution.py:90
  297.5 14.9 %collective-permute-start.53 = (bf16[1,1,288,384]{3,2,1,0:T(8,128)(2,1)S(1)}, bf16[1,1,288,384]{3,2,1,0:T(8,128)(2,1)S(1)}, u32[]{:S(2)}, u32[]{:S(2)}) collective-permute-start(bf16[1,1,288,384]{3,2,1,0:T(8,128)(2,1)S(1)} %get-tuple-element.206), channel_id=1, source_target_pairs={{0,1},{1,2},{2,3},{3,0},{4,5},{5,6},{6,7},{7,4},{8,9},{9,10},{10,1... | collective-permute-start | bytes 663560 | tf_op jit(solution)/shard_map/ppermute | solution.py:140
  298.3 21.1 %collective-permute-start.54 = (bf16[1,1,288,384]{3,2,1,0:T(8,128)(2,1)S(1)}, bf16[1,1,288,384]{3,2,1,0:T(8,128)(2,1)S(1)}, u32[]{:S(2)}, u32[]{:S(2)}) collective-permute-start(bf16[1,1,288,384]{3,2,1,0:T(8,128)(2,1)S(1)} %get-tuple-element.205), channel_id=1, source_target_pairs={{0,3},{1,0},{2,1},{3,2},{4,7},{5,4},{6,5},{7,6},{8,11},{9,8},{10,9... | collective-permute-start | bytes 663560 | tf_op jit(solution)/shard_map/ppermute | solution.py:140
  301.9 17.6 %collective-permute-start.50 = (bf16[128,1536]{1,0:T(8,128)(2,1)S(1)}, bf16[128,1536]{1,0:T(8,128)(2,1)S(1)}, u32[]{:S(2)}, u32[]{:S(2)}) collective-permute-start(bf16[128,1536]{1,0:T(8,128)(2,1)S(1)} %get-tuple-element.207), channel_id=1, source_target_pairs={{0,8},{8,0},{16,24},{24,16},{1,9},{9,1},{17,25},{25,17},{2,10},{10... | collective-permute-start | bytes 1179656 | tf_op jit(solution)/shard_map/ppermute | solution.py:90
  302.6 19.7 %collective-permute-start.51 = (bf16[128,1536]{1,0:T(8,128)(2,1)S(1)}, bf16[128,1536]{1,0:T(8,128)(2,1)S(1)}, u32[]{:S(2)}, u32[]{:S(2)}) collective-permute-start(bf16[128,1536]{1,0:T(8,128)(2,1)S(1)} %get-tuple-element.209), channel_id=1, source_target_pairs={{0,16},{8,24},{16,0},{24,8},{1,17},{9,25},{17,1},{25,9},{2,18},{10... | collective-permute-start | bytes 1179656 | tf_op jit(solution)/shard_map/ppermute | solution.py:90
  303.3 18.9 %collective-permute-start.52 = (bf16[128,1536]{1,0:T(8,128)(2,1)S(1)}, bf16[128,1536]{1,0:T(8,128)(2,1)S(1)}, u32[]{:S(2)}, u32[]{:S(2)}) collective-permute-start(bf16[128,1536]{1,0:T(8,128)(2,1)S(1)} %get-tuple-element.208), channel_id=1, source_target_pairs={{0,24},{8,16},{16,8},{24,0},{1,25},{9,17},{17,9},{25,1},{2,26},{10... | collective-permute-start | bytes 1179656 | tf_op jit(solution)/shard_map/ppermute | solution.py:90
  325.6 10.1 %collective-permute-start.58 = (bf16[1,1,288,384]{3,2,1,0:T(8,128)(2,1)S(1)}, bf16[1,1,288,384]{3,2,1,0:T(8,128)(2,1)S(1)}, u32[]{:S(2)}, u32[]{:S(2)}) collective-permute-start(bf16[1,1,288,384]{3,2,1,0:T(8,128)(2,1)S(1)} %get-tuple-element.138), channel_id=1, source_target_pairs={{0,1},{1,2},{2,3},{3,0},{4,5},{5,6},{6,7},{7,4},{8,9},{9,10},{10,1... | collective-permute-start | bytes 663560 | tf_op jit(solution)/shard_map/ppermute | solution.py:140
  325.6 12.0 %collective-permute-start.59 = (bf16[1,1,288,384]{3,2,1,0:T(8,128)(2,1)S(1)}, bf16[1,1,288,384]{3,2,1,0:T(8,128)(2,1)S(1)}, u32[]{:S(2)}, u32[]{:S(2)}) collective-permute-start(bf16[1,1,288,384]{3,2,1,0:T(8,128)(2,1)S(1)} %get-tuple-element.139), channel_id=1, source_target_pairs={{0,3},{1,0},{2,1},{3,2},{4,7},{5,4},{6,5},{7,6},{8,11},{9,8},{10,9... | collective-permute-start | bytes 663560 | tf_op jit(solution)/shard_map/ppermute | solution.py:140
  338.8 9.7 %collective-permute-start.62 = (bf16[4,48,1024]{2,1,0:T(8,128)(2,1)S(1)}, bf16[4,48,1024]{2,1,0:T(8,128)(2,1)S(1)}, u32[]{:S(2)}, u32[]{:S(2)}) collective-permute-start(bf16[4,48,1024]{2,1,0:T(8,128)(2,1)S(1)} %dynamic-slice_bitcast_fusion.1), channel_id=1, source_target_pairs={{0,4},{4,0},{1,5},{5,1},{2,6},{6,2},{3,7},{7,3},{8,12},{12,8},{9,1... | collective-permute-start | bytes 1179656 | tf_op jit(solution)/shard_map/ppermute | solution.py:87
  344.9 11.3 %collective-permute-start.61 = (bf16[1,1,288,384]{3,2,1,0:T(8,128)(2,1)S(1)}, bf16[1,1,288,384]{3,2,1,0:T(8,128)(2,1)S(1)}, u32[]{:S(2)}, u32[]{:S(2)}) collective-permute-start(bf16[1,1,288,384]{3,2,1,0:T(8,128)(2,1)S(1)} %get-tuple-element.141), channel_id=1, source_target_pairs={{0,3},{1,0},{2,1},{3,2},{4,7},{5,4},{6,5},{7,6},{8,11},{9,8},{10,9... | collective-permute-start | bytes 663560 | tf_op jit(solution)/shard_map/ppermute | solution.py:140
  (87 other events, 742.1 us)
Sparse Core Ops, SparseCore 0:
  17.8 68.0 all-gather.2
  219.7 32.6 reduce-scatter.2
  255.9 67.4 reduce-scatter.4
where the time goes:
time: 388 us; the launch traced here: 380 us
  waiting for transfers between devices  160 us (41%)
  starting transfers between devices  83.2 us (21%)
  matrix products  51.8 us (13%)
  local copies, waits for them, and re-layouts  35.9 us (9%)
  other arithmetic  33.8 us (9%)
  between operations  15.8 us (4%)
    ppermute x14, waiting for transfers between devices, along_z(): lax.ppermute(a, 'fsdp', [(i, (i + step) % rows_z) for i in range(rows_z)])  76.2 us
    ppermute x40, waiting for transfers between devices, chip_xor(): return lax.ppermute(a, 'chip', [(i, i ^ j) for i in range(chips)])  75.9 us
    ppermute x40, starting transfers between devices, chip_xor(): return lax.ppermute(a, 'chip', [(i, i ^ j) for i in range(chips)])  50.6 us
    ppermute x14, starting transfers between devices, along_z(): lax.ppermute(a, 'fsdp', [(i, (i + step) % rows_z) for i in range(rows_z)])  23 us
    dot_general x5, matrix products, mm(): return jnp.dot(a, b, preferred_element_type=f32)  15.5 us
    dot_general x5, matrix products, mm_nt(): return jnp.einsum('te,de->td', a, b, preferred_element_type=f32)  13.5 us
    dot_general x4, matrix products, mm_tn(): return jnp.einsum('td,te->de', a, b, preferred_element_type=f32)  12.2 us
  transfers between devices with their start and end apart: 76, of which 39 were waited for; matrix products, arithmetic and copies ran while one was open for 25% of the time, Pallas kernels for 0%

commit v1 on v0

--- a/solution.py
+++ b/solution.py
@@ -180,61 +180,38 @@
             whole = lax.dynamic_update_slice(whole, piece, (0, index, 0, column))
         return whole
 
-    owner = (chip * 2 + core) * rows_z + place
-    spot = chip * 2 + core
-    spots = chips * 2
-    gains = lax.dynamic_update_slice(
-        jnp.zeros((2, width), f32),
-        jnp.stack([attn_gain, mlp_gain]).astype(f32),
-        (0, owner * d_rows),
-    )
-    marks = lax.dynamic_update_slice(
-        jnp.zeros((4, spots * tok), f32),
-        jnp.concatenate([positions[:, 0], segments[:, 0]]).astype(f32),
-        (0, spot * tok),
-    )
-    table = jnp.concatenate([gains.reshape(-1), marks.reshape(-1)]).reshape(-1, 128)
-
-    def sum_chips(a):
-        bit = 1
-        while bit < chips:
-            a = a + chip_xor(a, bit)
-            bit *= 2
-        return a
-
-    def sum_z(a, bit=1, end=rows_z):
-        while bit < end:
-            a = a + lax.ppermute(a, "fsdp", [(i, i ^ bit) for i in range(rows_z)])
-            bit *= 2
-        return a
-
     def again(found, pieces):
         return [(piece,) + f[1:] for piece, f in zip(pieces, found)]
 
     def pieces_of(found):
         return [f[0] for f in found]
 
-    pack_qkv = chip_slices((w_query, w_key, w_value), (q_cols, kv_cols, kv_cols))
+    def scaled(gain, *weights):
+        return [(w.astype(f32) * gain.astype(f32)[:, None]).astype(bf16) for w in weights]
+
+    pack_qkv = chip_slices(
+        scaled(attn_gain, w_query, w_key, w_value), (q_cols, kv_cols, kv_cols)
+    )
     piece_qkv = exchange_chips(pack_qkv).reshape(-1, pack_qkv.shape[-1])
-    pair = jnp.stack([block_input[:, 0], out_cotangent[:, 0]], axis=1)
-    pair = jnp.concatenate([pick(pair, core), core_swap(pick(pair, 1 - core))], axis=1)
-    table = sum_chips(table + core_swap(table))
+    marks = jnp.stack([positions[:, 0] // 32, positions[:, 0] % 32, segments[:, 0]], axis=-1)
+    marks = jnp.pad(marks.astype(bf16), ((0, 0), (0, 0), (0, 125)))
+    pair = jnp.concatenate([out_cotangent[:, 0], block_input[:, 0], marks], axis=-1)
+    pair = jnp.concatenate([pick(pair, core), core_swap(pick(pair, 1 - core))])
     rows = jnp.concatenate([w_out, w_down])
-    rows = lax.all_gather(rows, "fsdp", axis=0)
+    gate_up = scaled(mlp_gain, w_gate, w_up)
     pack_gu = jnp.stack(
         [
-            jnp.concatenate([w[:, n * ff_cols : (n + 1) * ff_cols] for w in (w_gate, w_up)], axis=1)
+            jnp.concatenate([w[:, n * ff_cols : (n + 1) * ff_cols] for w in gate_up], axis=1)
             for n in range(2 * chips)
         ]
     ).reshape(chips, 2, d_rows, 2 * ff_cols)
-    pair, piece_qkv, table, pack_gu = tie(pair, piece_qkv, table, pack_gu)
-    x_low, dy_low = pair[0], pair[1]
+    pair, piece_qkv, pack_gu = tie(pair, piece_qkv, pack_gu)
+    dy_low, x_low = pair[:, :width], pair[:, width:]
 
     qkv_right, qkv_left = ring_first(piece_qkv)
     piece_gu = exchange_chips(pack_gu)
-    gains = sum_z(table.reshape(-1)[: 2 * width].reshape(2, width), 1, 2)
-    qkv_right, qkv_left, piece_gu, x_low, gains = tie(qkv_right, qkv_left, piece_gu, x_low, gains)
-    gains = sum_z(gains, 2, rows_z)
+    qkv_right, qkv_left, piece_gu, x_low, rows = tie(qkv_right, qkv_left, piece_gu, x_low, rows)
+    rows = lax.all_gather(rows, "fsdp", axis=0)
 
     near = [j for j in range(1, chips) if j & (j - 1) == 0]
     far = [j for j in range(1, chips) if j & (j - 1) != 0]
@@ -243,35 +220,26 @@
     piece_gu = core_pair(pick(piece_gu, core, 1), core_swap(pick(piece_gu, 1 - core, 1)), 1)
     piece_gu = piece_gu.reshape(2 * chips * d_rows, 2 * ff_cols)
     order = sorted(x_parts)
-    piece_gu, gains, *late = tie(piece_gu, gains, *[x_parts[j] for j in order], *pieces_of(found_qkv))
+    piece_gu, *late = tie(piece_gu, *[x_parts[j] for j in order], *pieces_of(found_qkv))
     x_parts = dict(zip(order, late))
     x_parts.update({j: chip_xor(x_parts[0], j) for j in far})
     x_all = jnp.concatenate([x_parts[j] for j in range(chips)])
     found_qkv = again(found_qkv, late[len(order) :])
     gu_right = along_z(piece_gu, 1)
-    marks = pick(table.reshape(-1)[2 * width :].reshape(2, 2, spots, tok), core, 1)
-    marks = jnp.concatenate(
-        [pick(marks, (chip ^ k) * 2 + (core ^ c), 1) for k in range(chips) for c in range(2)],
-        axis=1,
-    )
-    pos_all, seg_all = marks
+    marks = x_all[:, width : width + 3].astype(f32).T
+    pos_all, seg_all = marks[0] * 32.0 + marks[1], marks[2]
+    x_all, x_low = x_all[:, :width], x_low[:, :width]
     allowed = (seg_all[:, None] == seg_all[None, :]) & (pos_all[None, :] <= pos_all[:, None])
     cosine, sine = rope_tables(pos_all)
     w_qkv = assemble(found_qkv, chips)
     w_qkv = core_pair(w_qkv, core_swap(w_qkv), 1).reshape(width, -1)
-    w_qkv, x_all, dy_low, cosine, sine, allowed, gu_right, piece_gu, rows = tie(
-        w_qkv, x_all, dy_low, cosine, sine, allowed, gu_right, piece_gu, rows
-    )
-    along_out = rows[:, : w_out.shape[0]].reshape(-1, width)
-    along_down = rows[:, w_out.shape[0] :].reshape(-1, width)
-    gu_left = along_z(piece_gu, -1)
-    gain_one, gain_two = gains
+    w_qkv, x_all, dy_low, cosine, sine, allowed = tie(w_qkv, x_all, dy_low, cosine, sine, allowed)
     own = x_low.shape[0]
     seq = x_all.shape[0]
 
     dy_all = gather_chips(dy_low)
     x_full = x_all.astype(f32)
-    h_one = (x_full * rms_scale(x_full) * gain_one).astype(bf16)
+    h_one = (x_full * rms_scale(x_full)).astype(bf16)
     qkv = mm(h_one, w_qkv)
     q_rot = rotate(qkv[:, :q_cols].reshape(seq, kv_heads * 2, HEAD), cosine, sine)
     q_rot = q_rot.astype(bf16).reshape(seq, kv_heads, 2, HEAD)
@@ -279,6 +247,10 @@
         qkv[:, q_cols : q_cols + kv_cols].reshape(seq, kv_heads, HEAD), cosine, sine
     ).astype(bf16)
     value = qkv[:, q_cols + kv_cols :].astype(bf16).reshape(seq, kv_heads, HEAD)
+    q_rot, gu_right, piece_gu, rows = tie(q_rot, gu_right, piece_gu, rows)
+    gu_left = along_z(piece_gu, -1)
+    along_out = rows[:, : w_out.shape[0]].reshape(-1, width)
+    along_down = rows[:, w_out.shape[0] :].reshape(-1, width)
     out_w = both_cores(along_out).reshape(-1, width)
     scores = jnp.einsum("sgrh,tgh->grst", q_rot, k_rot, preferred_element_type=f32) * factor
     scores = jnp.where(allowed, scores, -1e30)
@@ -298,7 +270,7 @@
     w_gu = assemble(found_gu, 2 * chips).reshape(width, 2 * ff_cols)
     scale_two = rms_scale(middle)
     n_two = middle * scale_two
-    h_two = gather_chips((n_two * gain_two).astype(bf16))
+    h_two = gather_chips(n_two.astype(bf16))
     h_two, w_gu = tie(h_two, w_gu)
     h_both = jnp.concatenate([h_two, core_swap(h_two)])
     gu = mm(h_both, w_gu)
@@ -324,8 +296,7 @@
     g_gu = lax.psum_scatter(g_gu, "fsdp", scatter_dimension=0, tiled=True)
 
     dy_own = dy_low.astype(f32)
-    gain_two_part = jnp.sum(d_h_two * n_two, axis=0)
-    d_middle = dy_own + norm_back(d_h_two * gain_two, n_two, scale_two)
+    d_middle = dy_own + norm_back(d_h_two, n_two, scale_two)
     branch = gather_chips(d_middle.astype(bf16))
     partial = give_partial(act, along_down, mm)
     branch, partial, g_down = tie(branch, partial, g_down)
@@ -376,13 +347,10 @@
     d_h_one, *sums = tie(scatter_chips(d_h_one), *sums)
     scale_one = rms_scale(x_own)
     n_one = x_own * scale_one
-    gain_one_part = jnp.sum(d_h_one * n_one, axis=0)
-    gain_parts = jnp.stack([gain_one_part, gain_two_part])
-    gain_parts = sum_chips(gain_parts + core_swap(gain_parts))
-    gain_parts, *sums = tie(gain_parts, *scatter_window(g_rest, sums, 1))
+    sums = scatter_window(g_rest, sums, 1)
     sums = scatter_window(g_rest, sums, 2)
     g_rest = jnp.concatenate(sums, axis=-1).reshape(-1, cols_qkv)
-    d_input = (d_middle + norm_back(d_h_one * gain_one, n_one, scale_one)).astype(bf16)
+    d_input = (d_middle + norm_back(d_h_one, n_one, scale_one)).astype(bf16)
 
     def give_back(a):
         mine, theirs = a[:tok], core_swap(a[tok:])
@@ -402,24 +370,36 @@
     g_gu = core_pair(pick(g_gu, core, 1), core_swap(pick(g_gu, 1 - core, 1)), 1)
     g_gu = exchange_chips(g_gu)
     g_gate, g_up = spread_ff(g_gu[..., :ff_cols]), spread_ff(g_gu[..., ff_cols:])
-    gain_parts = sum_z(gain_parts)
-    gain_parts = lax.dynamic_slice_in_dim(gain_parts, owner * d_rows, d_rows, 1)
+
+    def of_gain(grads, weights):
+        return sum(jnp.sum(g * w.astype(f32), axis=1) for g, w in zip(grads, weights))
+
+    def by_gain(gain, grads):
+        return [g * gain.astype(f32)[:, None] for g in grads]
+
+    g_mlp_gain = of_gain((g_gate, g_up), (w_gate, w_up))
+    g_gate, g_up = by_gain(mlp_gain, (g_gate, g_up))
     result, d_input = give_back(result), give_back(d_input)
-    g_rest, g_gate, g_up, g_down, gain_parts, result, d_input = tie(
-        g_rest, g_gate, g_up, g_down, gain_parts, result, d_input
+    g_rest, g_gate, g_up, g_down, g_mlp_gain, result, d_input = tie(
+        g_rest, g_gate, g_up, g_down, g_mlp_gain, result, d_input
     )
     g_qkv = exchange_chips(g_rest[: chips * d_rows].reshape(chips, d_rows, cols_qkv))
     g_out = g_rest[chips * d_rows :].reshape(folds, d_rows, cols_qkv)
     g_out = jnp.transpose(g_out, (1, 0, 2)).reshape(d_rows, width).astype(f32)
+    g_query = spread(g_qkv, 0, q_cols)
+    g_key = spread(g_qkv, q_cols, kv_cols)
+    g_value = spread(g_qkv, q_cols + kv_cols, kv_cols)
+    g_attn_gain = of_gain((g_query, g_key, g_value), (w_query, w_key, w_value))
+    g_query, g_key, g_value = by_gain(attn_gain, (g_query, g_key, g_value))
     return (
         result,
         d_input,
-        gain_parts[0],
-        spread(g_qkv, 0, q_cols),
-        spread(g_qkv, q_cols, kv_cols),
-        spread(g_qkv, q_cols + kv_cols, kv_cols),
+        g_attn_gain,
+        g_query,
+        g_key,
+        g_value,
         g_out,
-        gain_parts[1],
+        g_mlp_gain,
         g_gate,
         g_up,
         g_down,

time: 388 us -> 364 us (0.938)
  starting transfers between devices: 83.2 us -> 70.6 us
  local copies, waits for them, and re-layouts: 35.9 us -> 28.4 us
    ppermute x14, waiting for transfers between devices: 76.2 us -> 55.1 us  [along_z(): lax.ppermute(a, 'fsdp', [(i, (i + step) % rows_z) for i in range(rows_z)])]
    all_gather x1, waiting for transfers between devices: 0.01 us -> 14.1 us  [on_device(): rows = lax.all_gather(rows, 'fsdp', axis=0)]
    ppermute x40 -> x36, waiting for transfers between devices: 75.9 us -> 84.5 us  [chip_xor(): return lax.ppermute(a, 'chip', [(i, i ^ j) for i in range(chips)])]
    ppermute x4 -> x0, starting transfers between devices: 7.39 us -> none  [sum_z(): a = a + lax.ppermute(a, 'fsdp', [(i, i ^ bit) for i in range(rows_z)])]
    ppermute x40 -> x36, starting transfers between devices: 50.6 us -> 44.5 us  [chip_xor(): return lax.ppermute(a, 'chip', [(i, i ^ j) for i in range(chips)])]
    unnamed x125 -> x116, local copies, waits for them, and re-layouts: 7.61 us -> 10.9 us
  transfers between devices with their start and end apart: 76 -> 66, of which waited for: 39 -> 43; matrix products, arithmetic and copies ran while one was open for 25% -> 23% of each run, Pallas kernels for 0% -> 0%
where the time goes in v1:
time: 364 us; the launch traced here: 357 us
  waiting for transfers between devices  157 us (43%)
  starting transfers between devices  70.6 us (19%)
  matrix products  49 us (13%)
  other arithmetic  36.1 us (10%)
  local copies, waits for them, and re-layouts  28.4 us (8%)
  between operations  15.8 us (4%)
    ppermute x36, waiting for transfers between devices, chip_xor(): return lax.ppermute(a, 'chip', [(i, i ^ j) for i in range(chips)])  84.5 us
    ppermute x14, waiting for transfers between devices, along_z(): lax.ppermute(a, 'fsdp', [(i, (i + step) % rows_z) for i in range(rows_z)])  55.1 us
    ppermute x36, starting transfers between devices, chip_xor(): return lax.ppermute(a, 'chip', [(i, i ^ j) for i in range(chips)])  44.5 us
    ppermute x14, starting transfers between devices, along_z(): lax.ppermute(a, 'fsdp', [(i, (i + step) % rows_z) for i in range(rows_z)])  24.7 us
    all_gather x1, waiting for transfers between devices, on_device(): rows = lax.all_gather(rows, 'fsdp', axis=0)  14.1 us
    dot_general x5, matrix products, mm(): return jnp.dot(a, b, preferred_element_type=f32)  13.8 us
    dot_general x5, matrix products, mm_nt(): return jnp.einsum('te,de->td', a, b, preferred_element_type=f32)  13.6 us
    dot_general x4, matrix products, mm_tn(): return jnp.einsum('td,te->de', a, b, preferred_element_type=f32)  12.3 us
  transfers between devices with their start and end apart: 66, of which 43 were waited for; matrix products, arithmetic and copies ran while one was open for 23% of the time, Pallas kernels for 0%

profile of v1, /device:TPU:0, one launch (start us, length us, event | category | flops | bytes accessed | tf_op | source)
XLA Modules:
  0.0 356.8 jit_solution(2613418557810242865)
XLA Ops:
  11.2 3.0 collective-permute-start.1
  18.6 2.5 collective-permute-done.3
  23.2 2.7 collective-permute-start.8
  28.3 2.2 collective-permute-start.5
  34.0 4.1 %collective-permute-done.4 = bf16[192,768]{1,0:T(8,128)(2,1)S(1)} collective-permute-done((bf16[192,768]{1,0:T(8,128)(2,1)S(1)}, bf16[192,768]{1,0:T(8,128)(2,1)S(1)}, u32[]{:S(2)}, u32[]{:S(2)}) %collective-permute-start.4) | collective-permute-done | bytes 294944 | tf_op jit(solution)/shard_map/ppermute | solution.py:140
  38.1 2.5 collective-permute-done.5
  45.4 2.7 collective-permute-start.13
  49.5 2.4 collective-permute-done.12
  59.2 7.7 %collective-permute-done.15 = bf16[128,1664]{1,0:T(8,128)(2,1)S(1)} collective-permute-done((bf16[128,1664]{1,0:T(8,128)(2,1)S(1)}, bf16[128,1664]{1,0:T(8,128)(2,1)S(1)}, u32[]{:S(2)}, u32[]{:S(2)}) %collective-permute-start.15) | collective-permute-done | bytes 426016 | tf_op jit(solution)/shard_map/ppermute | solution.py:90
  81.4 6.0 %collective-permute-done.18 = bf16[128,1536]{1,0:T(8,128)(2,1)} collective-permute-done((bf16[128,1536]{1,0:T(8,128)(2,1)S(1)}, bf16[128,1536]{1,0:T(8,128)(2,1)}, u32[]{:S(2)}, u32[]{:S(2)}) %collective-permute-start.18) | collective-permute-done | bytes 393248 | tf_op jit(solution)/shard_map/ppermute | solution.py:90
  88.8 2.5 pad_maximum_fusion.5
  91.3 3.9 %collective-permute-done.16 = bf16[384,1024]{1,0:T(8,128)(2,1)} collective-permute-done((bf16[384,1024]{1,0:T(8,128)(2,1)S(1)}, bf16[384,1024]{1,0:T(8,128)(2,1)}, u32[]{:S(2)}, u32[]{:S(2)}) %collective-permute-start.16) | collective-permute-done | bytes 786464 | tf_op jit(solution)/shard_map/ppermute | solution.py:140
  95.3 14.1 %all-gather.3.cloned.1.call-done = bf16[704,1536]{1,0:T(8,128)(2,1)} async-done(((bf16[176,1536]{1,0:T(8,128)(2,1)}), bf16[704,1536]{1,0:T(8,128)(2,1)}) %all-gather.3.cloned.1.call-update) | async-done | bytes 2162704 | tf_op jit(solution)/shard_map/all_gather | solution.py:214
  112.0 3.7 %fusion.105 = (f32[2,2,512]{2,1,0:T(2,128)S(1)}, f32[2,2,512,512]{2,3,1,0:T(8,128)}) fusion(pred[512,512]{0,1:T(8,128)(4,1)S(1)} %copy-done.42, bf16[512,2,2,96]{0,3,2,1:T(8,128)(2,1)S(1)} %pad_maximum_fusion.15, bf16[512,2,48]{0,2,1:T(8,128)(2,1)S(1)} %get-tuple-element.242, bf16[512,2,48]{0,2,1:T(8,128)(2,1)S(1)} %get-tuple-element.241), kind=kOutput, calls=%fused_computation.301 | convolution fusion | flops 205914624 | bytes 5054464 | tf_op jit(solution)/shard_map/sub | solution.py:257
  115.7 2.8 convolution_convert_fusion.6
  119.9 11.1 %collective-permute-done.21 = bf16[384,1024]{1,0:T(8,128)(2,1)} collective-permute-done((bf16[384,1024]{1,0:T(8,128)(2,1)S(1)}, bf16[384,1024]{1,0:T(8,128)(2,1)}, u32[]{:S(2)}, u32[]{:S(2)}) %collective-permute-start.21) | collective-permute-done | bytes 786464 | tf_op jit(solution)/shard_map/ppermute | solution.py:140
  137.9 6.3 %collective-permute-done.22 = bf16[128,1536]{1,0:T(8,128)(2,1)S(1)} collective-permute-done((bf16[128,1536]{1,0:T(8,128)(2,1)S(1)}, bf16[128,1536]{1,0:T(8,128)(2,1)S(1)}, u32[]{:S(2)}, u32[]{:S(2)}) %collective-permute-start.22) | collective-permute-done | bytes 393248 | tf_op jit(solution)/shard_map/ppermute | solution.py:90
  144.2 2.7 collective-permute-start.27
  146.9 6.4 %collective-permute-done.23 = bf16[128,1536]{1,0:T(8,128)(2,1)S(1)} collective-permute-done((bf16[128,1536]{1,0:T(8,128)(2,1)S(1)}, bf16[128,1536]{1,0:T(8,128)(2,1)S(1)}, u32[]{:S(2)}, u32[]{:S(2)}) %collective-permute-start.23) | collective-permute-done | bytes 393248 | tf_op jit(solution)/shard_map/ppermute | solution.py:90
  155.4 2.4 collective-permute-done.27
  164.6 5.5 %collective-permute-done.28 = bf16[128,1536]{1,0:T(8,128)(2,1)S(1)} collective-permute-done((bf16[128,1536]{1,0:T(8,128)(2,1)S(1)}, bf16[128,1536]{1,0:T(8,128)(2,1)S(1)}, u32[]{:S(2)}, u32[]{:S(2)}) %collective-permute-start.28) | collective-permute-done | bytes 393248 | tf_op jit(solution)/shard_map/ppermute | solution.py:90
  170.1 8.7 %collective-permute-done.29 = bf16[128,1536]{1,0:T(8,128)(2,1)S(1)} collective-permute-done((bf16[128,1536]{1,0:T(8,128)(2,1)S(1)}, bf16[128,1536]{1,0:T(8,128)(2,1)S(1)}, u32[]{:S(2)}, u32[]{:S(2)}) %collective-permute-start.29) | collective-permute-done | bytes 393248 | tf_op jit(solution)/shard_map/ppermute | solution.py:90
  179.2 3.2 collective-permute-done.31
  182.4 3.6 fusion.108
  186.0 3.5 multiply_convert_fusion.1
  189.6 3.1 convolution_convert_fusion.4
  192.9 5.2 %convolution_convert_fusion.3 = bf16[512,1536]{1,0:T(8,128)(2,1)} fusion(bf16[1024,512]{0,1:T(8,128)(2,1)} %get-tuple-element.119, bf16[1024,1536]{1,0:T(8,128)(2,1)} %copy-done.9), kind=kOutput, calls=%fused_computation.19 | convolution fusion | flops 1611399168 | bytes 5767168 | tf_op jit(solution)/shard_map/td,te->de/dot_general | solution.py:50
  198.0 3.7 %convolution_convert_fusion.2 = bf16[512,1536]{1,0:T(8,128)(2,1)} fusion(bf16[512,1536]{1,0:T(8,128)(2,1)} %bitcast.332, bf16[1024,512]{0,1:T(8,128)(2,1)} %get-tuple-element.119), kind=kOutput, calls=%fused_computation.18 | convolution fusion | flops 806092800 | bytes 3670016 | tf_op jit(solution)/shard_map/dot_general | solution.py:46
  202.4 4.7 %fusion.107 = (bf16[512,1536]{1,0:T(8,128)(2,1)S(1)}, f32[512,1536]{1,0:T(8,128)S(1)}) fusion(bf16[512,1536]{1,0:T(8,128)(2,1)} %collective-permute-done.32, bf16[1536,1024]{1,0:T(8,128)(2,1)} %bitcast.347, bf16[1024,512]{0,1:T(8,128)(2,1)} %copy-done.50, bf16[1024,512]{0,1:T(8,128)(2,1)} %copy-done.48), kind=kOutput, calls=%fused_computation.303 | convolution fusion | flops 1615069184 | bytes 11534336 | tf_op jit(solution)/shard_map/te,de->td/dot_general | solution.py:54
  210.8 4.7 %convolution_convert_fusion = bf16[1536,1024]{1,0:T(8,128)(2,1)S(1)} fusion(bf16[1024,1536]{1,0:T(8,128)(2,1)S(1)} %copy-done.24, bf16[1024,512]{0,1:T(8,128)(2,1)S(1)} %copy-done.49, bf16[1024,512]{0,1:T(8,128)(2,1)S(1)} %copy-done.51), kind=kOutput, calls=%fused_computation.10 | convolution fusion | flops 3226992640 | bytes 8388608 | tf_op jit(solution)/shard_map/td,te->de/dot_general | solution.py:50
  219.3 6.9 %collective-permute-done.34 = bf16[128,1536]{1,0:T(8,128)(2,1)S(1)} collective-permute-done((bf16[128,1536]{1,0:T(8,128)(2,1)S(1)}, bf16[128,1536]{1,0:T(8,128)(2,1)S(1)}, u32[]{:S(2)}, u32[]{:S(2)}) %collective-permute-start.34) | collective-permute-done | bytes 393248 | tf_op jit(solution)/shard_map/ppermute | solution.py:90
  232.0 4.1 %convert_add_fusion = f32[512,1536]{1,0:T(8,128)} fusion(bf16[512,1536]{1,0:T(8,128)(2,1)} %collective-permute-done.39, bf16[512,1536]{1,0:T(8,128)(2,1)S(1)} %bitcast.333, bf16[1024,512]{0,1:T(8,128)(2,1)S(1)} %copy-done.30), kind=kOutput, calls=%fused_computation.16 | convolution fusion | flops 806879232 | bytes 6815744 | tf_op jit(solution)/shard_map/dot_general | solution.py:46
  236.1 4.4 %collective-permute-done.36 = bf16[128,1536]{1,0:T(8,128)(2,1)S(1)} collective-permute-done((bf16[128,1536]{1,0:T(8,128)(2,1)S(1)}, bf16[128,1536]{1,0:T(8,128)(2,1)S(1)}, u32[]{:S(2)}, u32[]{:S(2)}) %collective-permute-start.36) | collective-permute-done | bytes 393248 | tf_op jit(solution)/shard_map/ppermute | solution.py:90
  240.5 7.2 %collective-permute-done.37 = bf16[128,1536]{1,0:T(8,128)(2,1)} collective-permute-done((bf16[128,1536]{1,0:T(8,128)(2,1)S(1)}, bf16[128,1536]{1,0:T(8,128)(2,1)}, u32[]{:S(2)}, u32[]{:S(2)}) %collective-permute-start.37) | collective-permute-done | bytes 393248 | tf_op jit(solution)/shard_map/ppermute | solution.py:90
  247.7 2.5 pad_maximum_fusion.7
  263.7 3.1 collective-permute-done.40
  267.4 2.5 collective-permute-start.44
  277.5 4.0 %collective-permute-start.49 = (bf16[1,1,288,384]{3,2,1,0:T(8,128)(2,1)S(1)}, bf16[1,1,288,384]{3,2,1,0:T(8,128)(2,1)S(1)}, u32[]{:S(2)}, u32[]{:S(2)}) collective-permute-start(bf16[1,1,288,384]{3,2,1,0:T(8,128)(2,1)S(1)} %get-tuple-element.193), channel_id=1, source_target_pairs={{0,3},{1,0},{2,1},{3,2},{4,7},{5,4},{6,5},{7,6},{8,11},{9,8},{10,9... | collective-permute-start | bytes 663560 | tf_op jit(solution)/shard_map/ppermute | solution.py:140
  282.9 2.2 collective-permute-start.46
  285.8 6.4 %collective-permute-done.48 = bf16[1,1,288,384]{3,2,1,0:T(8,128)(2,1)S(1)} collective-permute-done((bf16[1,1,288,384]{3,2,1,0:T(8,128)(2,1)S(1)}, bf16[1,1,288,384]{3,2,1,0:T(8,128)(2,1)S(1)}, u32[]{:S(2)}, u32[]{:S(2)}) %collective-permute-start.48) | collective-permute-done | bytes 221216 | tf_op jit(solution)/shard_map/ppermute | solution.py:140
  292.3 8.3 %collective-permute-done.49 = bf16[1,1,288,384]{3,2,1,0:T(8,128)(2,1)S(1)} collective-permute-done((bf16[1,1,288,384]{3,2,1,0:T(8,128)(2,1)S(1)}, bf16[1,1,288,384]{3,2,1,0:T(8,128)(2,1)S(1)}, u32[]{:S(2)}, u32[]{:S(2)}) %collective-permute-start.49) | collective-permute-done | bytes 221216 | tf_op jit(solution)/shard_map/ppermute | solution.py:140
  304.8 3.8 %collective-permute-start.52 = (bf16[1,1,288,384]{3,2,1,0:T(8,128)(2,1)S(1)}, bf16[1,1,288,384]{3,2,1,0:T(8,128)(2,1)S(1)}, u32[]{:S(2)}, u32[]{:S(2)}) collective-permute-start(bf16[1,1,288,384]{3,2,1,0:T(8,128)(2,1)S(1)} %get-tuple-element.133), channel_id=1, source_target_pairs={{0,3},{1,0},{2,1},{3,2},{4,7},{5,4},{6,5},{7,6},{8,11},{9,8},{10,9... | collective-permute-start | bytes 663560 | tf_op jit(solution)/shard_map/ppermute | solution.py:140
  310.6 4.3 %collective-permute-done.50 = bf16[1,1,288,384]{3,2,1,0:T(8,128)(2,1)S(1)} collective-permute-done((bf16[1,1,288,384]{3,2,1,0:T(8,128)(2,1)S(1)}, bf16[1,1,288,384]{3,2,1,0:T(8,128)(2,1)S(1)}, u32[]{:S(2)}, u32[]{:S(2)}) %collective-permute-start.50) | collective-permute-done | bytes 221216 | tf_op jit(solution)/shard_map/ppermute | solution.py:140
  314.9 2.4 collective-permute-done.52
  317.5 3.8 %collective-permute-start.53 = (bf16[1,1,288,384]{3,2,1,0:T(8,128)(2,1)S(1)}, bf16[1,1,288,384]{3,2,1,0:T(8,128)(2,1)S(1)}, u32[]{:S(2)}, u32[]{:S(2)}) collective-permute-start(bf16[1,1,288,384]{3,2,1,0:T(8,128)(2,1)S(1)} %get-tuple-element.190), channel_id=1, source_target_pairs={{0,3},{1,0},{2,1},{3,2},{4,7},{5,4},{6,5},{7,6},{8,11},{9,8},{10,9... | collective-permute-start | bytes 663560 | tf_op jit(solution)/shard_map/ppermute | solution.py:140
  325.0 2.6 collective-permute-done.51
  327.6 2.5 collective-permute-done.53
  344.0 2.6 collective-permute-done.62
  (387 shorter events, 129.8 us)
Async XLA Ops:
  7.2 102.1 %all-gather.3.cloned.1.call-start = ((), (), s32[]{:S(2)}) async-start(), calls=%async_computation.4 | async-start | bytes 2703360 | tf_op jit(solution)/shard_map/all_gather | solution.py:214
  22.9 9.6 %collective-permute-start.7 = (bf16[2,48,1024]{2,1,0:T(8,128)(2,1)S(1)}, bf16[2,48,1024]{2,1,0:T(8,128)(2,1)S(1)}, u32[]{:S(2)}, u32[]{:S(2)}) collective-permute-start(bf16[2,48,1024]{2,1,0:T(8,128)(2,1)S(1)} %get-tuple-element.231), channel_id=1, source_target_pairs={{0,16},{8,24},{16,0},{24,8},{1,17},{9,25},{17,1},{25,9},{2,18},{10... | collective-permute-start | bytes 589832 | tf_op jit(solution)/shard_map/ppermute | solution.py:90
  23.2 9.3 %collective-permute-start.8 = (bf16[2,48,1024]{2,1,0:T(8,128)(2,1)S(1)}, bf16[2,48,1024]{2,1,0:T(8,128)(2,1)}, u32[]{:S(2)}, u32[]{:S(2)}) collective-permute-start(bf16[2,48,1024]{2,1,0:T(8,128)(2,1)S(1)} %get-tuple-element.230), channel_id=1, source_target_pairs={{0,24},{8,16},{16,8},{24,0},{1,25},{9,17},{17,9},{25,1},{2,26},{10... | collective-permute-start | bytes 589832 | tf_op jit(solution)/shard_map/ppermute | solution.py:90
  26.7 11.3 %collective-permute-start.4 = (bf16[192,768]{1,0:T(8,128)(2,1)S(1)}, bf16[192,768]{1,0:T(8,128)(2,1)S(1)}, u32[]{:S(2)}, u32[]{:S(2)}) collective-permute-start(bf16[192,768]{1,0:T(8,128)(2,1)S(1)} %bitcast.380), channel_id=1, source_target_pairs={{0,1},{1,2},{2,3},{3,0},{4,5},{5,6},{6,7},{7,4},{8,9},{9,10},{10,1... | collective-permute-start | bytes 884744 | tf_op jit(solution)/shard_map/ppermute | solution.py:140
  28.3 12.3 %collective-permute-start.5 = (bf16[192,768]{1,0:T(8,128)(2,1)S(1)}, bf16[192,768]{1,0:T(8,128)(2,1)S(1)}, u32[]{:S(2)}, u32[]{:S(2)}) collective-permute-start(bf16[192,768]{1,0:T(8,128)(2,1)S(1)} %bitcast.381), channel_id=1, source_target_pairs={{0,3},{1,0},{2,1},{3,2},{4,7},{5,4},{6,5},{7,6},{8,11},{9,8},{10,9... | collective-permute-start | bytes 884744 | tf_op jit(solution)/shard_map/ppermute | solution.py:140
  41.4 12.6 %collective-permute-start.10 = (bf16[128,1664]{1,0:T(8,128)(2,1)S(1)}, bf16[128,1664]{1,0:T(8,128)(2,1)}, u32[]{:S(2)}, u32[]{:S(2)}) collective-permute-start(bf16[128,1664]{1,0:T(8,128)(2,1)S(1)} %slice.305), channel_id=1, source_target_pairs={{0,8},{8,0},{16,24},{24,16},{1,9},{9,1},{17,25},{25,17},{2,10},{10... | collective-permute-start | bytes 1277960 | tf_op jit(solution)/shard_map/ppermute | solution.py:90
  42.6 12.1 %collective-permute-start.11 = (bf16[128,1664]{1,0:T(8,128)(2,1)S(1)}, bf16[128,1664]{1,0:T(8,128)(2,1)}, u32[]{:S(2)}, u32[]{:S(2)}) collective-permute-start(bf16[128,1664]{1,0:T(8,128)(2,1)S(1)} %slice.305), channel_id=1, source_target_pairs={{0,16},{8,24},{16,0},{24,8},{1,17},{9,25},{17,1},{25,9},{2,18},{10... | collective-permute-start | bytes 1277960 | tf_op jit(solution)/shard_map/ppermute | solution.py:90
  48.1 202.0 %reduce-scatter.3.cloned.1.call-start = ((), (), s32[]{:S(2)}) async-start(), calls=%async_computation.2 | async-start | bytes 1966080 | tf_op jit(solution)/shard_map/reduce_scatter | solution.py:282
  54.7 12.1 %collective-permute-start.15 = (bf16[128,1664]{1,0:T(8,128)(2,1)S(1)}, bf16[128,1664]{1,0:T(8,128)(2,1)S(1)}, u32[]{:S(2)}, u32[]{:S(2)}) collective-permute-start(bf16[128,1664]{1,0:T(8,128)(2,1)S(1)} %slice.305), channel_id=1, source_target_pairs={{0,24},{8,16},{16,8},{24,0},{1,25},{9,17},{17,9},{25,1},{2,26},{10... | collective-permute-start | bytes 1277960 | tf_op jit(solution)/shard_map/ppermute | solution.py:90
  56.1 12.7 %collective-permute-start.14 = (bf16[4,4,48,768]{3,2,1,0:T(8,128)(2,1)S(1)}, bf16[4,4,48,768]{3,2,1,0:T(8,128)(2,1)S(1)}, u32[]{:S(2)}, u32[]{:S(2)}) collective-permute-start(bf16[4,4,48,768]{3,2,1,0:T(8,128)(2,1)S(1)} %constant_dynamic-update-slice_fusion.11), channel_id=1, source_target_pairs={{0,4},{4,0},{1,5},{5,1},{2,6},{6,2},{3,7},{7,3},{8,12},{12,8},{9,1... | collective-permute-start | bytes 3538952 | tf_op jit(solution)/shard_map/ppermute | solution.py:87
  56.2 39.1 %collective-permute-start.16 = (bf16[384,1024]{1,0:T(8,128)(2,1)S(1)}, bf16[384,1024]{1,0:T(8,128)(2,1)}, u32[]{:S(2)}, u32[]{:S(2)}) collective-permute-start(bf16[384,1024]{1,0:T(8,128)(2,1)S(1)} %bitcast.338), channel_id=1, source_target_pairs={{0,1},{1,2},{2,3},{3,0},{4,5},{5,6},{6,7},{7,4},{8,9},{9,10},{10,1... | collective-permute-start | bytes 2359304 | tf_op jit(solution)/shard_map/ppermute | solution.py:140
  69.2 12.2 %collective-permute-start.17 = (bf16[128,1536]{1,0:T(8,128)(2,1)S(1)}, bf16[128,1536]{1,0:T(8,128)(2,1)}, u32[]{:S(2)}, u32[]{:S(2)}) collective-permute-start(bf16[128,1536]{1,0:T(8,128)(2,1)S(1)} %slice.309), channel_id=1, source_target_pairs={{0,8},{8,0},{16,24},{24,16},{1,9},{9,1},{17,25},{25,17},{2,10},{10... | collective-permute-start | bytes 1179656 | tf_op jit(solution)/shard_map/ppermute | solution.py:90
  70.0 17.4 %collective-permute-start.18 = (bf16[128,1536]{1,0:T(8,128)(2,1)S(1)}, bf16[128,1536]{1,0:T(8,128)(2,1)}, u32[]{:S(2)}, u32[]{:S(2)}) collective-permute-start(bf16[128,1536]{1,0:T(8,128)(2,1)S(1)} %slice.309), channel_id=1, source_target_pairs={{0,16},{8,24},{16,0},{24,8},{1,17},{9,25},{17,1},{25,9},{2,18},{10... | collective-permute-start | bytes 1179656 | tf_op jit(solution)/shard_map/ppermute | solution.py:90
  71.4 17.4 %collective-permute-start.19 = (bf16[128,1536]{1,0:T(8,128)(2,1)S(1)}, bf16[128,1536]{1,0:T(8,128)(2,1)}, u32[]{:S(2)}, u32[]{:S(2)}) collective-permute-start(bf16[128,1536]{1,0:T(8,128)(2,1)S(1)} %slice.309), channel_id=1, source_target_pairs={{0,24},{8,16},{16,8},{24,0},{1,25},{9,17},{17,9},{25,1},{2,26},{10... | collective-permute-start | bytes 1179656 | tf_op jit(solution)/shard_map/ppermute | solution.py:90
  110.6 20.5 %collective-permute-start.21 = (bf16[384,1024]{1,0:T(8,128)(2,1)S(1)}, bf16[384,1024]{1,0:T(8,128)(2,1)}, u32[]{:S(2)}, u32[]{:S(2)}) collective-permute-start(bf16[384,1024]{1,0:T(8,128)(2,1)S(1)} %bitcast.339), channel_id=1, source_target_pairs={{0,3},{1,0},{2,1},{3,2},{4,7},{5,4},{6,5},{7,6},{8,11},{9,8},{10,9... | collective-permute-start | bytes 2359304 | tf_op jit(solution)/shard_map/ppermute | solution.py:140
  131.0 22.7 %collective-permute-start.25 = (bf16[512,1536]{1,0:T(8,128)(2,1)}, bf16[512,1536]{1,0:T(8,128)(2,1)S(1)}, u32[]{:S(2)}, u32[]{:S(2)}) collective-permute-start(bf16[512,1536]{1,0:T(8,128)(2,1)} %pad_maximum_fusion.5), channel_id=1, source_target_pairs={{0,4},{4,0},{1,5},{5,1},{2,6},{6,2},{3,7},{7,3},{8,12},{12,8},{9,1... | collective-permute-start | bytes 4718600 | tf_op jit(solution)/shard_map/ppermute | solution.py:87
  132.2 12.1 %collective-permute-start.22 = (bf16[128,1536]{1,0:T(8,128)(2,1)S(1)}, bf16[128,1536]{1,0:T(8,128)(2,1)S(1)}, u32[]{:S(2)}, u32[]{:S(2)}) collective-permute-start(bf16[128,1536]{1,0:T(8,128)(2,1)S(1)} %get-tuple-element.204), channel_id=1, source_target_pairs={{0,8},{8,0},{16,24},{24,16},{1,9},{9,1},{17,25},{25,17},{2,10},{10... | collective-permute-start | bytes 1179656 | tf_op jit(solution)/shard_map/ppermute | solution.py:90
  133.7 19.7 %collective-permute-start.23 = (bf16[128,1536]{1,0:T(8,128)(2,1)S(1)}, bf16[128,1536]{1,0:T(8,128)(2,1)S(1)}, u32[]{:S(2)}, u32[]{:S(2)}) collective-permute-start(bf16[128,1536]{1,0:T(8,128)(2,1)S(1)} %get-tuple-element.206), channel_id=1, source_target_pairs={{0,16},{8,24},{16,0},{24,8},{1,17},{9,25},{17,1},{25,9},{2,18},{10... | collective-permute-start | bytes 1179656 | tf_op jit(solution)/shard_map/ppermute | solution.py:90
  135.2 18.2 %collective-permute-start.24 = (bf16[128,1536]{1,0:T(8,128)(2,1)S(1)}, bf16[128,1536]{1,0:T(8,128)(2,1)S(1)}, u32[]{:S(2)}, u32[]{:S(2)}) collective-permute-start(bf16[128,1536]{1,0:T(8,128)(2,1)S(1)} %get-tuple-element.205), channel_id=1, source_target_pairs={{0,24},{8,16},{16,8},{24,0},{1,25},{9,17},{17,9},{25,1},{2,26},{10... | collective-permute-start | bytes 1179656 | tf_op jit(solution)/shard_map/ppermute | solution.py:90
  136.7 18.6 %collective-permute-start.26 = (bf16[384,512]{1,0:T(8,128)(2,1)S(1)}, bf16[384,512]{1,0:T(8,128)(2,1)S(1)}, u32[]{:S(2)}, u32[]{:S(2)}) collective-permute-start(bf16[384,512]{1,0:T(8,128)(2,1)S(1)} %slice.327), channel_id=1, source_target_pairs={{0,1},{1,2},{2,3},{3,0},{4,5},{5,6},{6,7},{7,4},{8,9},{9,10},{10,1... | collective-permute-start | bytes 1179656 | tf_op jit(solution)/shard_map/ppermute | solution.py:140
  144.2 13.5 %collective-permute-start.27 = (bf16[384,512]{1,0:T(8,128)(2,1)S(1)}, bf16[384,512]{1,0:T(8,128)(2,1)S(1)}, u32[]{:S(2)}, u32[]{:S(2)}) collective-permute-start(bf16[384,512]{1,0:T(8,128)(2,1)S(1)} %slice.328), channel_id=1, source_target_pairs={{0,3},{1,0},{2,1},{3,2},{4,7},{5,4},{6,5},{7,6},{8,11},{9,8},{10,9... | collective-permute-start | bytes 1179656 | tf_op jit(solution)/shard_map/ppermute | solution.py:140
  158.0 12.1 %collective-permute-start.28 = (bf16[128,1536]{1,0:T(8,128)(2,1)S(1)}, bf16[128,1536]{1,0:T(8,128)(2,1)S(1)}, u32[]{:S(2)}, u32[]{:S(2)}) collective-permute-start(bf16[128,1536]{1,0:T(8,128)(2,1)S(1)} %multiply_convert_fusion.3), channel_id=1, source_target_pairs={{0,8},{8,0},{16,24},{24,16},{1,9},{9,1},{17,25},{25,17},{2,10},{10... | collective-permute-start | bytes 1179656 | tf_op jit(solution)/shard_map/ppermute | solution.py:90
  159.6 19.2 %collective-permute-start.29 = (bf16[128,1536]{1,0:T(8,128)(2,1)S(1)}, bf16[128,1536]{1,0:T(8,128)(2,1)S(1)}, u32[]{:S(2)}, u32[]{:S(2)}) collective-permute-start(bf16[128,1536]{1,0:T(8,128)(2,1)S(1)} %multiply_convert_fusion.3), channel_id=1, source_target_pairs={{0,16},{8,24},{16,0},{24,8},{1,17},{9,25},{17,1},{25,9},{2,18},{10... | collective-permute-start | bytes 1179656 | tf_op jit(solution)/shard_map/ppermute | solution.py:90
  161.0 17.7 %collective-permute-start.30 = (bf16[128,1536]{1,0:T(8,128)(2,1)S(1)}, bf16[128,1536]{1,0:T(8,128)(2,1)S(1)}, u32[]{:S(2)}, u32[]{:S(2)}) collective-permute-start(bf16[128,1536]{1,0:T(8,128)(2,1)S(1)} %multiply_convert_fusion.3), channel_id=1, source_target_pairs={{0,24},{8,16},{16,8},{24,0},{1,25},{9,17},{17,9},{25,1},{2,26},{10... | collective-permute-start | bytes 1179656 | tf_op jit(solution)/shard_map/ppermute | solution.py:90
  192.7 9.7 %collective-permute-start.32 = (bf16[512,1536]{1,0:T(8,128)(2,1)}, bf16[512,1536]{1,0:T(8,128)(2,1)}, u32[]{:S(2)}, u32[]{:S(2)}) collective-permute-start(bf16[512,1536]{1,0:T(8,128)(2,1)} %convolution_convert_fusion.4), channel_id=1, source_target_pairs={{0,4},{4,0},{1,5},{5,1},{2,6},{6,2},{3,7},{7,3},{8,12},{12,8},{9,1... | collective-permute-start | bytes 4718600 | tf_op jit(solution)/shard_map/ppermute | solution.py:87
  201.8 30.3 %collective-permute-start.39 = (bf16[512,1536]{1,0:T(8,128)(2,1)}, bf16[512,1536]{1,0:T(8,128)(2,1)}, u32[]{:S(2)}, u32[]{:S(2)}) collective-permute-start(bf16[512,1536]{1,0:T(8,128)(2,1)} %convolution_convert_fusion.2), channel_id=1, source_target_pairs={{0,4},{4,0},{1,5},{5,1},{2,6},{6,2},{3,7},{7,3},{8,12},{12,8},{9,1... | collective-permute-start | bytes 4718600 | tf_op jit(solution)/shard_map/ppermute | solution.py:87
  202.2 106.5 %reduce-scatter.5.cloned.1.call-start = ((), (), s32[]{:S(2)}) async-start(), calls=%async_computation.3 | async-start | bytes 3932160 | tf_op jit(solution)/shard_map/reduce_scatter | solution.py:296
  207.2 12.1 %collective-permute-start.33 = (bf16[128,1536]{1,0:T(8,128)(2,1)S(1)}, bf16[128,1536]{1,0:T(8,128)(2,1)S(1)}, u32[]{:S(2)}, u32[]{:S(2)}) collective-permute-start(bf16[128,1536]{1,0:T(8,128)(2,1)S(1)} %get-tuple-element.201), channel_id=1, source_target_pairs={{0,8},{8,0},{16,24},{24,16},{1,9},{9,1},{17,25},{25,17},{2,10},{10... | collective-permute-start | bytes 1179656 | tf_op jit(solution)/shard_map/ppermute | solution.py:90
  208.5 17.7 %collective-permute-start.34 = (bf16[128,1536]{1,0:T(8,128)(2,1)S(1)}, bf16[128,1536]{1,0:T(8,128)(2,1)S(1)}, u32[]{:S(2)}, u32[]{:S(2)}) collective-permute-start(bf16[128,1536]{1,0:T(8,128)(2,1)S(1)} %get-tuple-element.203), channel_id=1, source_target_pairs={{0,16},{8,24},{16,0},{24,8},{1,17},{9,25},{17,1},{25,9},{2,18},{10... | collective-permute-start | bytes 1179656 | tf_op jit(solution)/shard_map/ppermute | solution.py:90
  209.3 18.5 %collective-permute-start.35 = (bf16[128,1536]{1,0:T(8,128)(2,1)S(1)}, bf16[128,1536]{1,0:T(8,128)(2,1)S(1)}, u32[]{:S(2)}, u32[]{:S(2)}) collective-permute-start(bf16[128,1536]{1,0:T(8,128)(2,1)S(1)} %get-tuple-element.202), channel_id=1, source_target_pairs={{0,24},{8,16},{16,8},{24,0},{1,25},{9,17},{17,9},{25,1},{2,26},{10... | collective-permute-start | bytes 1179656 | tf_op jit(solution)/shard_map/ppermute | solution.py:90
  228.5 12.1 %collective-permute-start.36 = (bf16[128,1536]{1,0:T(8,128)(2,1)S(1)}, bf16[128,1536]{1,0:T(8,128)(2,1)S(1)}, u32[]{:S(2)}, u32[]{:S(2)}) collective-permute-start(bf16[128,1536]{1,0:T(8,128)(2,1)S(1)} %fusion.94), channel_id=1, source_target_pairs={{0,8},{8,0},{16,24},{24,16},{1,9},{9,1},{17,25},{25,17},{2,10},{10... | collective-permute-start | bytes 1179656 | tf_op jit(solution)/shard_map/ppermute | solution.py:90
  229.4 18.3 %collective-permute-start.37 = (bf16[128,1536]{1,0:T(8,128)(2,1)S(1)}, bf16[128,1536]{1,0:T(8,128)(2,1)}, u32[]{:S(2)}, u32[]{:S(2)}) collective-permute-start(bf16[128,1536]{1,0:T(8,128)(2,1)S(1)} %fusion.94), channel_id=1, source_target_pairs={{0,16},{8,24},{16,0},{24,8},{1,17},{9,25},{17,1},{25,9},{2,18},{10... | collective-permute-start | bytes 1179656 | tf_op jit(solution)/shard_map/ppermute | solution.py:90
  230.9 16.8 %collective-permute-start.38 = (bf16[128,1536]{1,0:T(8,128)(2,1)S(1)}, bf16[128,1536]{1,0:T(8,128)(2,1)}, u32[]{:S(2)}, u32[]{:S(2)}) collective-permute-start(bf16[128,1536]{1,0:T(8,128)(2,1)S(1)} %fusion.94), channel_id=1, source_target_pairs={{0,24},{8,16},{16,8},{24,0},{1,25},{9,17},{17,9},{25,1},{2,26},{10... | collective-permute-start | bytes 1179656 | tf_op jit(solution)/shard_map/ppermute | solution.py:90
  257.8 9.0 %collective-permute-start.40 = (bf16[128,1536]{1,0:T(8,128)(2,1)S(1)}, bf16[128,1536]{1,0:T(8,128)(2,1)S(1)}, u32[]{:S(2)}, u32[]{:S(2)}) collective-permute-start(bf16[128,1536]{1,0:T(8,128)(2,1)S(1)} %get-tuple-element.200), channel_id=1, source_target_pairs={{0,8},{8,0},{16,24},{24,16},{1,9},{9,1},{17,25},{25,17},{2,10},{10... | collective-permute-start | bytes 1179656 | tf_op jit(solution)/shard_map/ppermute | solution.py:90
  260.0 10.2 %collective-permute-start.42 = (bf16[192,1536]{1,0:T(8,128)(2,1)S(1)}, bf16[192,1536]{1,0:T(8,128)(2,1)S(1)}, u32[]{:S(2)}, u32[]{:S(2)}) collective-permute-start(bf16[192,1536]{1,0:T(8,128)(2,1)S(1)} %dynamic-slice_bitcast_fusion), channel_id=1, source_target_pairs={{0,4},{4,0},{1,5},{5,1},{2,6},{6,2},{3,7},{7,3},{8,12},{12,8},{9,1... | collective-permute-start | bytes 1769480 | tf_op jit(solution)/shard_map/ppermute | solution.py:87
  267.4 9.4 %collective-permute-start.44 = (bf16[128,1536]{1,0:T(8,128)(2,1)S(1)}, bf16[128,1536]{1,0:T(8,128)(2,1)S(1)}, u32[]{:S(2)}, u32[]{:S(2)}) collective-permute-start(bf16[128,1536]{1,0:T(8,128)(2,1)S(1)} %get-tuple-element.129), channel_id=1, source_target_pairs={{0,24},{8,16},{16,8},{24,0},{1,25},{9,17},{17,9},{25,1},{2,26},{10... | collective-permute-start | bytes 1179656 | tf_op jit(solution)/shard_map/ppermute | solution.py:90
  277.4 14.9 %collective-permute-start.48 = (bf16[1,1,288,384]{3,2,1,0:T(8,128)(2,1)S(1)}, bf16[1,1,288,384]{3,2,1,0:T(8,128)(2,1)S(1)}, u32[]{:S(2)}, u32[]{:S(2)}) collective-permute-start(bf16[1,1,288,384]{3,2,1,0:T(8,128)(2,1)S(1)} %get-tuple-element.194), channel_id=1, source_target_pairs={{0,1},{1,2},{2,3},{3,0},{4,5},{5,6},{6,7},{7,4},{8,9},{9,10},{10,1... | collective-permute-start | bytes 663560 | tf_op jit(solution)/shard_map/ppermute | solution.py:140
  277.5 23.1 %collective-permute-start.49 = (bf16[1,1,288,384]{3,2,1,0:T(8,128)(2,1)S(1)}, bf16[1,1,288,384]{3,2,1,0:T(8,128)(2,1)S(1)}, u32[]{:S(2)}, u32[]{:S(2)}) collective-permute-start(bf16[1,1,288,384]{3,2,1,0:T(8,128)(2,1)S(1)} %get-tuple-element.193), channel_id=1, source_target_pairs={{0,3},{1,0},{2,1},{3,2},{4,7},{5,4},{6,5},{7,6},{8,11},{9,8},{10,9... | collective-permute-start | bytes 663560 | tf_op jit(solution)/shard_map/ppermute | solution.py:140
  281.8 18.8 %collective-permute-start.45 = (bf16[128,1536]{1,0:T(8,128)(2,1)S(1)}, bf16[128,1536]{1,0:T(8,128)(2,1)S(1)}, u32[]{:S(2)}, u32[]{:S(2)}) collective-permute-start(bf16[128,1536]{1,0:T(8,128)(2,1)S(1)} %get-tuple-element.195), channel_id=1, source_target_pairs={{0,8},{8,0},{16,24},{24,16},{1,9},{9,1},{17,25},{25,17},{2,10},{10... | collective-permute-start | bytes 1179656 | tf_op jit(solution)/shard_map/ppermute | solution.py:90
  282.9 19.4 %collective-permute-start.46 = (bf16[128,1536]{1,0:T(8,128)(2,1)S(1)}, bf16[128,1536]{1,0:T(8,128)(2,1)S(1)}, u32[]{:S(2)}, u32[]{:S(2)}) collective-permute-start(bf16[128,1536]{1,0:T(8,128)(2,1)S(1)} %get-tuple-element.197), channel_id=1, source_target_pairs={{0,16},{8,24},{16,0},{24,8},{1,17},{9,25},{17,1},{25,9},{2,18},{10... | collective-permute-start | bytes 1179656 | tf_op jit(solution)/shard_map/ppermute | solution.py:90
  285.1 17.9 %collective-permute-start.47 = (bf16[128,1536]{1,0:T(8,128)(2,1)S(1)}, bf16[128,1536]{1,0:T(8,128)(2,1)S(1)}, u32[]{:S(2)}, u32[]{:S(2)}) collective-permute-start(bf16[128,1536]{1,0:T(8,128)(2,1)S(1)} %get-tuple-element.196), channel_id=1, source_target_pairs={{0,24},{8,16},{16,8},{24,0},{1,25},{9,17},{17,9},{25,1},{2,26},{10... | collective-permute-start | bytes 1179656 | tf_op jit(solution)/shard_map/ppermute | solution.py:90
  304.8 10.1 %collective-permute-start.50 = (bf16[1,1,288,384]{3,2,1,0:T(8,128)(2,1)S(1)}, bf16[1,1,288,384]{3,2,1,0:T(8,128)(2,1)S(1)}, u32[]{:S(2)}, u32[]{:S(2)}) collective-permute-start(bf16[1,1,288,384]{3,2,1,0:T(8,128)(2,1)S(1)} %get-tuple-element.132), channel_id=1, source_target_pairs={{0,1},{1,2},{2,3},{3,0},{4,5},{5,6},{6,7},{7,4},{8,9},{9,10},{10,1... | collective-permute-start | bytes 663560 | tf_op jit(solution)/shard_map/ppermute | solution.py:140
  304.8 12.6 %collective-permute-start.52 = (bf16[1,1,288,384]{3,2,1,0:T(8,128)(2,1)S(1)}, bf16[1,1,288,384]{3,2,1,0:T(8,128)(2,1)S(1)}, u32[]{:S(2)}, u32[]{:S(2)}) collective-permute-start(bf16[1,1,288,384]{3,2,1,0:T(8,128)(2,1)S(1)} %get-tuple-element.133), channel_id=1, source_target_pairs={{0,3},{1,0},{2,1},{3,2},{4,7},{5,4},{6,5},{7,6},{8,11},{9,8},{10,9... | collective-permute-start | bytes 663560 | tf_op jit(solution)/shard_map/ppermute | solution.py:140
  309.8 11.5 %collective-permute-start.54 = (bf16[4,48,1024]{2,1,0:T(8,128)(2,1)S(1)}, bf16[4,48,1024]{2,1,0:T(8,128)(2,1)S(1)}, u32[]{:S(2)}, u32[]{:S(2)}) collective-permute-start(bf16[4,48,1024]{2,1,0:T(8,128)(2,1)S(1)} %dynamic-slice_bitcast_fusion.3), channel_id=1, source_target_pairs={{0,4},{4,0},{1,5},{5,1},{2,6},{6,2},{3,7},{7,3},{8,12},{12,8},{9,1... | collective-permute-start | bytes 1179656 | tf_op jit(solution)/shard_map/ppermute | solution.py:87
  317.4 10.2 %collective-permute-start.51 = (bf16[1,1,288,384]{3,2,1,0:T(8,128)(2,1)S(1)}, bf16[1,1,288,384]{3,2,1,0:T(8,128)(2,1)S(1)}, u32[]{:S(2)}, u32[]{:S(2)}) collective-permute-start(bf16[1,1,288,384]{3,2,1,0:T(8,128)(2,1)S(1)} %get-tuple-element.189), channel_id=1, source_target_pairs={{0,1},{1,2},{2,3},{3,0},{4,5},{5,6},{6,7},{7,4},{8,9},{9,10},{10,1... | collective-permute-start | bytes 663560 | tf_op jit(solution)/shard_map/ppermute | solution.py:140
  317.5 12.6 %collective-permute-start.53 = (bf16[1,1,288,384]{3,2,1,0:T(8,128)(2,1)S(1)}, bf16[1,1,288,384]{3,2,1,0:T(8,128)(2,1)S(1)}, u32[]{:S(2)}, u32[]{:S(2)}) collective-permute-start(bf16[1,1,288,384]{3,2,1,0:T(8,128)(2,1)S(1)} %get-tuple-element.190), channel_id=1, source_target_pairs={{0,3},{1,0},{2,1},{3,2},{4,7},{5,4},{6,5},{7,6},{8,11},{9,8},{10,9... | collective-permute-start | bytes 663560 | tf_op jit(solution)/shard_map/ppermute | solution.py:140
  321.4 8.8 %collective-permute-start.55 = (bf16[2,48,1024]{2,1,0:T(8,128)(2,1)S(1)}, bf16[2,48,1024]{2,1,0:T(8,128)(2,1)S(1)}, u32[]{:S(2)}, u32[]{:S(2)}) collective-permute-start(bf16[2,48,1024]{2,1,0:T(8,128)(2,1)S(1)} %get-tuple-element.226), channel_id=1, source_target_pairs={{0,8},{8,0},{16,24},{24,16},{1,9},{9,1},{17,25},{25,17},{2,10},{10... | collective-permute-start | bytes 589832 | tf_op jit(solution)/shard_map/ppermute | solution.py:90
  323.8 9.0 %collective-permute-start.57 = (bf16[2,48,1024]{2,1,0:T(8,128)(2,1)S(1)}, bf16[2,48,1024]{2,1,0:T(8,128)(2,1)S(1)}, u32[]{:S(2)}, u32[]{:S(2)}) collective-permute-start(bf16[2,48,1024]{2,1,0:T(8,128)(2,1)S(1)} %get-tuple-element.228), channel_id=1, source_target_pairs={{0,24},{8,16},{16,8},{24,0},{1,25},{9,17},{17,9},{25,1},{2,26},{10... | collective-permute-start | bytes 589832 | tf_op jit(solution)/shard_map/ppermute | solution.py:90
  (72 other events, 517.3 us)
Sparse Core Ops, SparseCore 0:
  48.3 61.0 all-gather.2
  202.3 32.6 reduce-scatter.2
  237.3 68.6 reduce-scatter.4
